TPU v7x, 128 devices: a whole 4x4x4 slice. The times are simulated.
128 devices in a mesh: gx: 8 (over x, y_lo), gy: 16 (over z, y_hi, core).
Axes of the slice: x: 4, y: 4 (y_hi: 2, y_lo: 2; y = y_hi * 2 + y_lo), z: 4, core: 2. Of those that a mesh axis runs over, the one named last changes fastest.
Arguments:
- xi_coarse: float32 [1024, 2048], P('gx', 'gy'), may hold values from -6 to 6
- xi_middle: float32 [2048, 4096], P('gx', 'gy'), may hold values from -6 to 6
- xi_fine: float32 [4096, 8192], P('gx', 'gy'), may hold values from -6 to 6
- coef_middle: bfloat16 [4, 9, 1024, 2048], P(None, None, 'gx', 'gy'), may hold values from -1.1953125 to 1.1953125
- coef_fine: bfloat16 [4, 9, 2048, 4096], P(None, None, 'gx', 'gy'), may hold values from -1.1953125 to 1.1953125
- kern_u: bfloat16 [8, 32, 1024, 512], P('gx', 'gy'), may hold values from -0.25 to 0.25
- kern_v: bfloat16 [8, 32, 1024, 512], P('gx', 'gy'), may hold values from -0.25 to 0.25
- vis_data: bfloat16 [8, 32, 1024, 1024], P('gx', 'gy'), may hold values from -6 to 6
- facet_tiles: int32 [8, 32, 2], P('gx', 'gy'), may hold values from 0 to 15, as said below
- facet_weight: float32 [8, 32, 2], P('gx', 'gy'), may hold values from 0.5 to 1.5
- facet_count: int32 [8, 32], P('gx', 'gy'), may hold values from 256 to 1024, as said below
Outputs:
- grad_coarse: float32 [1024, 2048], P('gx', 'gy')
- grad_middle: float32 [2048, 4096], P('gx', 'gy')
- grad_fine: float32 [4096, 8192], P('gx', 'gy')
- potential: float32 [], replicated
Inputs may be any that keep to these rules, and one draw needn't show every extreme that they name: `facet_tiles`: every tile column of a row is named by some facet of that row. `facet_count`: bins 0 to the count minus one of a facet are used.
All inputs are finite; a program needn't handle non-finite values.
Results may differ from a plain program's by a relative error of at most 0.0085.
Values may be sent and summed in bfloat16 or wider, within the bound.
A program may use at most 320 MiB of HBM per device.

v0:
```python
import jax
import jax.numpy as jnp
from jax import lax
from jax.sharding import PartitionSpec as P

inv_noise = 0.125


def extended(x, sides, width):
    for axis, dim in sides:
        size, length = (lax.axis_size(axis), x.shape[dim])
        up = [(i, (i + 1) % size) for i in range(size - 1)]
        down = [(j, i) for i, j in up]
        last = lax.slice_in_dim(x, length - width, length, axis=dim)
        leading = lax.slice_in_dim(x, 0, width, axis=dim)
        before = lax.ppermute(last, axis, up)
        after = lax.ppermute(leading, axis, down)
        x = jnp.concatenate([before, x, after], axis=dim)
    return x


def as_sent(x):

    def short(part):
        return part.astype(jnp.bfloat16) if part.dtype == jnp.float32 else part

    return jax.tree.map(short, x)


def alternate(quads, rows, cols):
    return quads.reshape(2, 2, rows, cols).transpose(2, 0, 3, 1).reshape(2 * rows, 2 * cols)


def widen(field):
    return extended(field, (("gx", 0), ("gy", 1)), 1)


def refine(field, weights):
    rows, cols = (weights.shape[2], weights.shape[3])
    padded = widen(field)
    quads = []
    for child in range(4):
        total = jnp.zeros((rows, cols), jnp.float32)
        for near in range(9):
            shift_r, shift_c = (near // 3 - 1, near % 3 - 1)
            window = padded[1 + shift_r : 1 + shift_r + rows, 1 + shift_c : 1 + shift_c + cols]
            total = total + weights[child, near].astype(jnp.float32) * window
        quads.append(total)
    return alternate(jnp.stack(quads), rows, cols)


def back(grad, weights):
    rows, cols = (weights.shape[2], weights.shape[3])
    quads = grad.reshape(rows, 2, cols, 2).transpose(1, 3, 0, 2).reshape(4, rows, cols)
    parts = []
    for near in range(9):
        total = jnp.zeros((rows, cols), jnp.float32)
        for child in range(4):
            total = total + weights[child, near].astype(jnp.float32) * quads[child]
        parts.append(total)
    padded = extended(as_sent(jnp.stack(parts)), (("gx", 1), ("gy", 2)), 1)
    result = jnp.zeros((rows, cols), jnp.float32)
    for near in range(9):
        shift_r, shift_c = (near // 3 - 1, near % 3 - 1)
        result = (
            result
            + padded[near, 1 - shift_r : 1 - shift_r + rows, 1 - shift_c : 1 - shift_c + cols]
        )
    return result


def body(
    xi_coarse,
    xi_middle,
    xi_fine,
    coef_middle,
    coef_fine,
    kern_u,
    kern_v,
    vis_data,
    facet_tiles,
    facet_weight,
    facet_count,
):
    level_middle = refine(xi_coarse, coef_middle) + xi_middle
    level_fine = refine(level_middle, coef_fine) + xi_fine
    sky_tile = level_fine.astype(jnp.bfloat16)
    side = sky_tile.shape[0]
    bins = vis_data.shape[2]
    mine = lax.axis_index("gy")
    lists = facet_tiles[0]
    weights = facet_weight[0]
    piece = lax.all_gather(sky_tile, "gy", axis=1, tiled=True)
    count = piece.shape[1] // side
    tile_ids = jnp.arange(count, dtype=jnp.int32)
    mixing = jnp.sum(
        weights[:, :, None] * (lists[:, :, None] == tile_ids[None, None, :]).astype(jnp.float32),
        axis=1,
    )
    blocks = piece.reshape(side, count, side).astype(jnp.float32)
    sums = jnp.sum(mixing[:, None, :, None] * blocks[None], axis=2)
    amp = jnp.einsum(
        "fbx,fxy->fby", kern_u[0], sums.astype(jnp.bfloat16), preferred_element_type=jnp.float32
    ).astype(jnp.bfloat16)
    vis = jnp.einsum("fby,fcy->fbc", amp, kern_v[0], preferred_element_type=jnp.float32)
    live = (jnp.arange(bins, dtype=jnp.int32)[None, :] < facet_count[0][:, None]).astype(
        jnp.float32
    )
    resid = live[:, :, None] * (vis - vis_data[0].astype(jnp.float32))
    likelihood = 0.5 * inv_noise * jnp.sum(resid * resid)
    dvis = (inv_noise * resid).astype(jnp.bfloat16)
    damp = jnp.einsum("fbc,fcy->fby", dvis, kern_v[0], preferred_element_type=jnp.float32).astype(
        jnp.bfloat16
    )
    dsum = jnp.einsum("fbx,fby->fxy", kern_u[0], damp, preferred_element_type=jnp.float32)
    grads = lax.all_gather(dsum[None].astype(jnp.bfloat16), "gy", axis=1, tiled=True).astype(
        jnp.float32
    )
    piece_list = lax.all_gather(facet_tiles, "gy", axis=1, tiled=True)
    piece_weight = lax.all_gather(
        facet_weight.astype(jnp.bfloat16), "gy", axis=1, tiled=True
    ).astype(jnp.float32)
    mixing = jnp.sum(piece_weight[0] * (piece_list[0] == mine).astype(jnp.float32), axis=1)
    dsky = jnp.zeros((side, side), jnp.float32) + jnp.sum(mixing[:, None, None] * grads[0], axis=0)
    grad_fine = dsky + xi_fine
    dmiddle = back(dsky, coef_fine)
    grad_middle = dmiddle + xi_middle
    grad_coarse = back(dmiddle, coef_middle) + xi_coarse
    prior = 0.5 * (
        jnp.sum(xi_coarse * xi_coarse) + jnp.sum(xi_middle * xi_middle) + jnp.sum(xi_fine * xi_fine)
    )
    total = lax.psum(prior + likelihood, ("gx", "gy"))
    cells = lax.axis_size("gx") * lax.axis_size("gy") * side * side
    return (grad_coarse, grad_middle, grad_fine, total / cells)


def solution(mesh):
    placed = (
        P("gx", "gy"),
        P("gx", "gy"),
        P("gx", "gy"),
        P(None, None, "gx", "gy"),
        P(None, None, "gx", "gy"),
        P("gx", "gy", None, None),
        P("gx", "gy", None, None),
        P("gx", "gy", None, None),
        P("gx", "gy", None),
        P("gx", "gy", None),
        P("gx", "gy"),
    )
    return jax.shard_map(
        body,
        mesh=mesh,
        in_specs=placed,
        out_specs=(P("gx", "gy"), P("gx", "gy"), P("gx", "gy"), P()),
        check_vma=False,
    )
```

profile of v0, /device:TPU:0, one launch (start us, length us, event | category | flops | bytes accessed | tf_op | source)
XLA Modules:
  0.0 684.0 jit_solution(10225893192071008046)
XLA Ops:
  20.8 5.0 collective-permute-done.3
  29.4 8.6 %copy.47 = f32[2,2,128,128]{1,3,0,2:T(8,128)} copy(f32[2,2,128,128]{3,2,1,0:T(8,128)S(1)} %bitcast.1339) | data formatting | bytes 524288 | tf_op jit(solution)/shard_map/reshape | solution.py:31
  38.1 12.7 %reshape.1143 = f32[256,256]{1,0:T(8,128)S(1)} reshape(f32[128,2,128,2]{3,2,1,0:T(8,128)} %bitcast.1326) | data formatting | bytes 524288 | tf_op jit(solution)/shard_map/reshape | solution.py:31
  56.7 4.2 collective-permute-done.5
  61.0 5.0 collective-permute-start.6
  77.9 32.2 %copy.48 = f32[2,2,256,256]{1,3,0,2:T(8,128)} copy(f32[2,2,256,256]{3,2,1,0:T(8,128)S(1)} %bitcast.1338) | data formatting | bytes 2097152 | tf_op jit(solution)/shard_map/reshape | solution.py:31
  110.1 47.0 %reshape.1145 = f32[512,512]{1,0:T(8,128)S(1)} reshape(f32[256,2,256,2]{3,2,1,0:T(8,128)} %bitcast.90) | data formatting | bytes 2097152 | tf_op jit(solution)/shard_map/reshape | solution.py:31
  160.4 83.7 %all-gather.4.cloned.1.call-done = bf16[512,8192]{1,0:T(8,128)(2,1)} async-done(((bf16[512,512]{1,0:T(8,128)(2,1)}), bf16[512,8192]{1,0:T(8,128)(2,1)}) %all-gather.4.cloned.1.call-update) | async-done | bytes 8388624 | tf_op jit(solution)/shard_map/all_gather | solution.py:93
  244.1 17.4 %copy.67 = f32[64,8,16,512]{3,2,1,0:T(8,128)} copy(bf16[64,8,16,512]{3,1,2,0:T(8,128)(2,1)} %bitcast.1337) | data formatting | bytes 25165824
  261.5 15.8 %multiply_reduce_fusion = bf16[2,512,512]{2,1,0:T(8,128)(2,1)S(1)} fusion(f32[512,16,512]{2,1,0:T(8,128)} %bitcast.1325, f32[2,16]{1,0:T(2,128)S(1)} %fusion.332), kind=kLoop, calls=%fused_computation.2 | loop fusion | flops 16252928 | bytes 17825920 | tf_op jit(solution)/shard_map/reduce_sum | solution.py:101
  277.3 9.4 %multiply_reduce_fusion.1 = (f32[]{:T(128)}, f32[2,1024,1024]{2,1,0:T(8,128)}) fusion(bf16[1,2,1024,1024]{3,2,1,0:T(8,128)(2,1)} %param.18, f32[2,1024]{1,0:T(2,128)S(1)} %compare_convert_fusion, bf16[1,2,1024,512]{3,2,1,0:T(8,128)(2,1)} %param.17, bf16[1,2,1024,512]{3,2,1,0:T(8,128)(2,1)S(1)} %copy-done, bf16[2,512,512]{2,1,0:T(8,128)(2,1)S(1)} %multiply_reduce_fusion), kind=kOutput, calls=%fused_computation.5 | convolution fusion | flops 3232759808 | bytes 17833988 | tf_op jit(solution)/shard_map/fby,fcy->fbc/dot_general | solution.py:105
  286.7 8.8 %fusion.24 = bf16[2,512,512]{1,2,0:T(8,128)(2,1)S(1)} fusion(bf16[1,2,1024,512]{3,2,1,0:T(8,128)(2,1)S(1)} %copy-done, f32[2,1024,1024]{2,1,0:T(8,128)} %get-tuple-element.43, bf16[1,2,1024,1024]{3,2,1,0:T(8,128)(2,1)} %param.18, f32[2,1024]{1,0:T(2,128)S(1)} %compare_convert_fusion, bf16[1,2,1024,512]{3,2,1,0:T(8,128)(2,1)} %param.17), kind=kOutput, calls=%fused_computation.21 | convolution fusion | flops 3233284096 | bytes 17833984 | tf_op jit(solution)/shard_map/fbx,fby->fxy/dot_general | solution.py:115
  296.9 20.0 %all_gather.13 = bf16[1,32,2]{2,0,1:T(2,128)(2,1)S(1)} all-gather(bf16[1,2,2]{2,0,1:T(2,128)(2,1)S(1)} %convert_element_type.1561), channel_id=1, replica_groups=mesh['gx'=8,'gy'=16] {'gy'}, dimensions={1}, use_global_device_ids=true | all-gather | bytes 136 | tf_op jit(solution)/shard_map/all_gather | solution.py:120
  316.9 21.8 %all_gather.12 = s32[1,32,2]{2,0,1:T(1,128)S(1)} all-gather(s32[1,2,2]{2,0,1:T(1,128)S(1)} %bitcast.1341), channel_id=1, replica_groups=mesh['gx'=8,'gy'=16] {'gy'}, dimensions={1}, use_global_device_ids=true | all-gather | bytes 272 | tf_op jit(solution)/shard_map/all_gather | solution.py:119
  339.0 64.4 %all-gather.6.cloned.1.call-done = bf16[32,512,512]{2,1,0:T(8,128)(2,1)} async-done(((bf16[2,512,512]{2,1,0:T(8,128)(2,1)}), bf16[32,512,512]{2,1,0:T(8,128)(2,1)}) %all-gather.6.cloned.1.call-update) | async-done | bytes 16777232 | tf_op jit(solution)/shard_map/all_gather | solution.py:116
  403.4 7.7 %fusion = f32[512,512]{1,0:T(8,128)S(1)} fusion(bf16[32,512,512]{2,1,0:T(8,128)(2,1)} %all-gather.6.cloned.1.call-done, f32[32]{0:T(128)S(1)} %fusion.331), kind=kLoop, calls=%fused_computation.1 | loop fusion | flops 24903680 | bytes 17825920 | tf_op jit(solution)/shard_map/reduce_sum | solution.py:124
  411.1 68.4 %reshape.1146 = f32[256,2,256,2]{3,2,1,0:T(8,128)} reshape(f32[512,512]{1,0:T(8,128)S(1)} %fusion) | data formatting | bytes 2097152 | tf_op jit(solution)/shard_map/reshape | solution.py:54
  479.4 36.8 %copy.55 = f32[2,2,256,256]{3,2,1,0:T(8,128)S(1)} copy(f32[2,2,256,256]{1,3,0,2:T(8,128)} %bitcast.95) | data formatting | bytes 2097152 | tf_op jit(solution)/shard_map/transpose | solution.py:54
  530.9 4.5 collective-permute-done.9
  547.6 18.1 %reshape.1326 = f32[128,2,128,2]{3,2,1,0:T(8,128)} reshape(f32[1,256,256]{2,1,0:T(8,128)S(1)} %get-tuple-element.13) | data formatting | bytes 524288 | tf_op jit(solution)/shard_map/add | solution.py:66
  565.7 10.1 %copy.60 = f32[2,2,128,128]{3,2,1,0:T(8,128)S(1)} copy(f32[2,2,128,128]{1,3,0,2:T(8,128)} %bitcast.1327) | data formatting | bytes 524288 | tf_op jit(solution)/shard_map/transpose | solution.py:54
  576.2 4.8 collective-permute-start.12
  582.4 4.2 collective-permute-done.13
  597.4 69.4 %psum.7 = f32[]{:T(128)} all-reduce(f32[]{:T(128)S(6)} %add.664), channel_id=1, replica_groups=mesh['gx'=8,'gy'=16] {'gx','gy'}, use_global_device_ids=true, to_apply=%region_8.0 | all-reduce | flops 1 | bytes 8 | tf_op jit(solution)/shard_map/psum | solution.py:132
  (112 shorter events, 84.9 us)
Async XLA Ops:
  7.2 270.1 %copy-start = (bf16[1,2,1024,512]{3,2,1,0:T(8,128)(2,1)S(1)}, bf16[1,2,1024,512]{3,2,1,0:T(8,128)(2,1)}, u32[]{:S(2)}) copy-start(bf16[1,2,1024,512]{3,2,1,0:T(8,128)(2,1)} %param.16) | copy-start | bytes 6291460
  7.2 22.0 %copy-start.4 = (f32[128,128]{1,0:T(8,128)S(1)}, f32[128,128]{1,0:T(8,128)}, u32[]{:S(2)}) copy-start(f32[128,128]{1,0:T(8,128)} %param.11) | copy-start | bytes 196612
  7.2 21.9 %copy-start.2 = (bf16[4,9,128,128]{3,2,1,0:T(8,128)(2,1)S(1)}, bf16[4,9,128,128]{3,2,1,0:T(8,128)(2,1)}, u32[]{:S(2)}) copy-start(bf16[4,9,128,128]{3,2,1,0:T(8,128)(2,1)} %param.14) | copy-start | bytes 3538948
  7.2 236.9 %all-gather.4.cloned.1.call-start = ((), (), s32[]{:S(2)}) async-start(), calls=%async_computation | async-start | bytes 8912896 | tf_op jit(solution)/shard_map/all_gather | solution.py:93
  8.1 5.0 collective-permute-start
  11.8 5.5 collective-permute-start.1
  18.2 2.6 collective-permute-start.2
  19.5 6.3 collective-permute-start.3
  38.1 12.7 %copy-start.7 = (f32[256,256]{1,0:T(8,128)S(1)}, f32[256,256]{1,0:T(8,128)}, u32[]{:S(2)}) copy-start(f32[256,256]{1,0:T(8,128)} %param.12) | copy-start | bytes 786436
  51.5 5.2 collective-permute-start.4
  55.4 5.5 collective-permute-start.5
  61.0 6.3 collective-permute-start.6
  65.9 4.7 collective-permute-start.7
  160.0 243.3 %all-gather.6.cloned.1.call-start = ((), (), s32[]{:S(2)}) async-start(), calls=%async_computation.1 | async-start | bytes 17825792 | tf_op jit(solution)/shard_map/all_gather | solution.py:116
  527.1 3.9 collective-permute-start.8
  529.6 5.9 collective-permute-start.9
  538.5 4.9 collective-permute-start.10
  540.3 3.9 collective-permute-start.11
  565.7 10.1 %copy-start.3 = (bf16[4,9,128,128]{3,2,1,0:T(8,128)(2,1)S(1)}, bf16[4,9,128,128]{3,2,1,0:T(8,128)(2,1)}, u32[]{:S(2)}) copy-start(bf16[4,9,128,128]{3,2,1,0:T(8,128)(2,1)} %param.14) | copy-start | bytes 3538948
  576.2 19.6 %copy-start.5 = (bf16[9,128,128]{2,1,0:T(8,128)(2,1)}, bf16[9,128,128]{2,1,0:T(8,128)(2,1)S(1)}, u32[]{:S(2)}) copy-start(bf16[9,128,128]{2,1,0:T(8,128)(2,1)S(1)} %constant_dynamic-update-slice_fusion.1) | copy-start | bytes 884740
  576.2 6.1 collective-permute-start.12
  581.0 5.5 collective-permute-start.13
  587.6 86.3 %collective-permute-start.14 = (bf16[9,130,1]{2,1,0:T(8,128)(2,1)}, bf16[9,130,1]{2,1,0:T(8,128)(2,1)}, u32[]{:S(2)}, u32[]{:S(2)}) collective-permute-start(bf16[9,130,1]{2,1,0:T(8,128)(2,1)} %get-tuple-element.24), channel_id=1, source_target_pairs={{1,0},{2,1},{3,2},{4,3},{5,4},{6,5},{7,6},{8,7},{9,8},{10,9},{11,1... | collective-permute-start | bytes 7028 | tf_op jit(solution)/shard_map/ppermute | solution.py:17
  588.9 85.1 %collective-permute-start.15 = (bf16[9,130,1]{2,1,0:T(8,128)(2,1)}, bf16[9,130,1]{2,1,0:T(8,128)(2,1)}, u32[]{:S(2)}, u32[]{:S(2)}) collective-permute-start(bf16[9,130,1]{2,1,0:T(8,128)(2,1)} %get-tuple-element.25), channel_id=1, source_target_pairs={{0,1},{1,2},{2,3},{3,4},{4,5},{5,6},{6,7},{7,8},{8,9},{9,10},{10,1... | collective-permute-start | bytes 7028 | tf_op jit(solution)/shard_map/ppermute | solution.py:16
  (5 other events, 18.8 us)
Sparse Core Ops, SparseCore 0:
  160.1 83.9 all-gather.3
  297.0 106.3 all-gather.5
where the time goes:
time: 693 us; the launch traced here: 684 us
  local copies, waits for them, and re-layouts  265 us (38%)
  waiting for transfers between devices  174 us (25%)
  blocking collectives  111 us (16%)
  other arithmetic  58 us (8%)
  starting transfers between devices  38.5 us (6%)
  between operations  19.3 us (3%)
  matrix products  18.2 us (3%)
    reshape x4, local copies, waits for them, and re-layouts, alternate(): quads.reshape(2, 2, rows, cols).transpose(2, 0, 3, 1)  101 us
    all_gather x1, waiting for transfers between devices, body(): piece = lax.all_gather(sky_tile, 'gy', axis=1, tiled=True)  83.7 us
    psum x1, blocking collectives, body(): total = lax.psum(prior + likelihood, ('gx', 'gy'))  69.4 us
    reshape x1, local copies, waits for them, and re-layouts, back(): grad.reshape(rows, 2, cols, 2).transpose(1, 3, 0, 2).reshape(4, rows, cols)  68.4 us
    all_gather x1, waiting for transfers between devices, body(): lax.all_gather(dsum[None].astype(jnp.bfloat16), 'gy', axis=1, tiled=True)  64.4 us
    transpose x2, local copies, waits for them, and re-layouts, back(): grad.reshape(rows, 2, cols, 2).transpose(1, 3, 0, 2).reshape(4, rows, cols)  46.8 us
    ppermute x8, starting transfers between devices, extended(): before = lax.ppermute(last, axis, up)  27.9 us
    ppermute x8, waiting for transfers between devices, extended(): after = lax.ppermute(leading, axis, down)  25.4 us
  transfers between devices with their start and end apart: 18, of which 10 were waited for; matrix products, arithmetic and copies ran while one was open for 1% of the time, Pallas kernels for 0%

commit v1 on v0

v1 whole, which is shorter than its diff:
```python
import functools

import jax
import jax.numpy as jnp
from jax import lax
from jax.experimental import pallas as pl
from jax.experimental.pallas import tpu as pltpu
from jax.sharding import PartitionSpec as P

inv_noise = 0.125
MESH = pl.DeviceIdType.MESH
ROW, LANE = 8, 128
SIDES = [(dx, dy) for dx in (-1, 0, 1) for dy in (-1, 0, 1) if (dx, dy) != (0, 0)]


def f32dot(a, b, contract):
    return lax.dot_general(a, b, ((contract[:1], contract[1:]), ((), ())), preferred_element_type=jnp.float32)


def split(x):
    high = x.astype(jnp.bfloat16)
    return high, (x - high.astype(jnp.float32)).astype(jnp.bfloat16)


def strip(side, size, edge, near):
    if side == 0:
        return edge, size
    if near:
        return (edge, edge) if side < 0 else (size, edge)
    return (0, edge) if side < 0 else (edge + size, edge)


def region(dx, dy, rows, cols, near):
    return (pl.ds(*strip(dx, rows, ROW, near)), pl.ds(*strip(dy, cols, LANE, near)))


class Halo:
    def __init__(self, src, dst, rows, cols, near, send, recv, at):
        gx, gy, m, n = at
        self.dst, self.at = dst, at
        self.copies = []
        for i, (dx, dy) in enumerate(SIDES):
            self.copies.append(
                pltpu.make_async_remote_copy(
                    src_ref=src.at[region(dx, dy, rows, cols, near)],
                    dst_ref=dst.at[region(-dx, -dy, rows, cols, False)],
                    send_sem=send.at[i],
                    recv_sem=recv.at[i],
                    device_id=(lax.rem(gx + dx + m, m), lax.rem(gy + dy + n, n)),
                    device_id_type=MESH,
                )
            )

    def start(self):
        for c in self.copies:
            c.start()

    def wait(self):
        for c in self.copies:
            c.wait()
        gx, gy, m, n = self.at
        dst = self.dst
        rows, cols = dst.shape
        dst[0:ROW, :] = jnp.where(gx > 0, dst[0:ROW, :], 0.0)
        dst[rows - ROW : rows, :] = jnp.where(gx < m - 1, dst[rows - ROW : rows, :], 0.0)
        dst[:, 0:LANE] = jnp.where(gy > 0, dst[:, 0:LANE], 0.0)
        dst[:, cols - LANE : cols] = jnp.where(gy < n - 1, dst[:, cols - LANE : cols], 0.0)


class Exchange:
    def __init__(self, src, dst, send, recv, at, slab):
        self.src, self.dst, self.send, self.recv, self.at, self.slab = src, dst, send, recv, at, slab

    def copy(self, k):
        gx, gy, m, n = self.at
        peer = lax.rem(gy + k, n)
        return pltpu.make_async_remote_copy(
            src_ref=self.src.at[pl.ds(pl.multiple_of(peer * self.slab, self.slab), self.slab), :],
            dst_ref=self.dst.at[pl.ds(pl.multiple_of(gy * self.slab, self.slab), self.slab), :],
            send_sem=self.send.at[k],
            recv_sem=self.recv.at[k],
            device_id=(gx, peer),
            device_id_type=MESH,
        )

    def start(self):
        gx, gy, m, n = self.at

        @pl.loop(1, n)
        def _(k):
            self.copy(k).start()

        own = pl.ds(pl.multiple_of(gy * self.slab, self.slab), self.slab)
        self.dst[own, :] = self.src[own, :]

    def wait(self):
        @pl.loop(1, self.at[3])
        def _(k):
            self.copy(k).wait()


def spread(ref):
    size = ref.shape[0]
    half = size // 2
    row = lax.broadcasted_iota(jnp.int32, (half, size), 0)
    col = lax.broadcasted_iota(jnp.int32, (half, size), 1)
    ref[0:half, :] = jnp.where(col == 2 * row, 1.0, 0.0).astype(jnp.bfloat16)
    ref[half:size, :] = jnp.where(col == 2 * row + 1, 1.0, 0.0).astype(jnp.bfloat16)


def refine(pad, wins, coef, rolled, high, low, size, rows):
    width = size + 2 * LANE
    for dj in (-1, 0, 1):
        value = pad[...]
        if dj:
            value = pltpu.roll(value, (-dj) % width, 1)
        rolled[...] = value[:, LANE : LANE + size]
        for di in (-1, 0, 1):
            wins[3 * (di + 1) + dj + 1] = rolled[ROW + di : ROW + di + size, :]

    @pl.loop(0, size // rows)
    def _(step):
        at = pl.multiple_of(step * rows, rows)
        here = pl.ds(at, rows)
        totals = [None] * 4
        for near in range(9):
            window = wins[near, here, :]
            for child in range(4):
                term = coef[child, near, here, :].astype(jnp.float32) * window
                totals[child] = term if near == 0 else totals[child] + term
        for child in range(4):
            a, b = child // 2, child % 2
            there = pl.ds(pl.multiple_of(a * size + at, rows), rows)
            high[there, b * size : (b + 1) * size], low[there, b * size : (b + 1) * size] = split(totals[child])


def interleave(high, low, matrix, laced, size):
    for a in (0, 1):
        rows = slice(a * size, (a + 1) * size)
        value = f32dot(high[rows, :], matrix[...], (1, 0)) + f32dot(low[rows, :], matrix[...], (1, 0))
        for c in range(2 * size // LANE):
            laced[c, pl.ds(a, size, stride=2), :] = value[:, c * LANE : (c + 1) * LANE]


def parent_terms(quads, coef, shifted, result, size, rows):
    width = size + 2 * LANE
    tall = size + 4 * ROW
    for d in range(3):
        shifted[d, 0 : 2 * ROW, :] = jnp.zeros((2 * ROW, width), jnp.float32)
        shifted[d, tall - 2 * ROW : tall, :] = jnp.zeros((2 * ROW, width), jnp.float32)

    @pl.loop(0, size // rows)
    def _(step):
        at = pl.multiple_of(step * rows, rows)
        here = pl.ds(at, rows)
        quad = [
            quads[pl.ds(pl.multiple_of(a * size + at, rows), rows), b * size : (b + 1) * size]
            for a in (0, 1)
            for b in (0, 1)
        ]
        blank = jnp.zeros((rows, LANE), jnp.float32)
        for d in range(3):
            total = None
            for j in range(3):
                part = None
                for child in range(4):
                    term = coef[child, 3 * d + j, here, :].astype(jnp.float32) * quad[child]
                    part = term if child == 0 else part + term
                part = jnp.concatenate([blank, part, blank], axis=1)
                if j != 1:
                    part = pltpu.roll(part, (j - 1) % width, 1)
                total = part if j == 0 else total + part
            shifted[d, pl.ds(pl.multiple_of(at + 2 * ROW, ROW), rows), :] = total

    high = tall - 2 * ROW
    result[...] = (
        shifted[1, ROW : ROW + high, :]
        + shifted[2, ROW - 1 : ROW - 1 + high, :]
        + shifted[0, ROW + 1 : ROW + 1 + high, :]
    )


def fold_rim(result, rim, size):
    full_r, full_c = slice(ROW, ROW + size), slice(LANE, LANE + size)
    for rim_r, own_r in ((slice(0, ROW), slice(ROW, 2 * ROW)), (slice(ROW + size, 2 * ROW + size), slice(size, size + ROW))):
        result[own_r, full_c] += rim[rim_r, full_c]
    for rim_c, own_c in (
        (slice(0, LANE), slice(LANE, 2 * LANE)),
        (slice(LANE + size, 2 * LANE + size), slice(size, size + LANE)),
    ):
        result[full_r, own_c] += rim[full_r, rim_c]
        for rim_r, own_r in (
            (slice(0, ROW), slice(ROW, 2 * ROW)),
            (slice(ROW + size, 2 * ROW + size), slice(size, size + ROW)),
        ):
            result[own_r, own_c] += rim[rim_r, rim_c]


def squares(x):
    return jnp.sum(x * x, axis=0, keepdims=True)


def fold_lanes(x):
    total = x[:, 0:LANE]
    for c in range(1, x.shape[1] // LANE):
        total = total + x[:, c * LANE : (c + 1) * LANE]
    return total


def kernel(
    m, n, cells,
    xi_c, xi_m, xi_f, co_m, co_f, k_u, k_v, v_d, meta, counts,
    g_c, g_m, g_f, pot,
    pad_c, pad_m, xm, xf, cm, cf, ku, kv, vd,
    roll_c, roll_m, win_c, win_m, hi_c, lo_c, hi_m, lo_m, lace_c, lace_m, mat_c, mat_m,
    metas, mix_hi, mix_lo, sky, tiles, sums, fsum, dsum, dslab, back_b, dsky,
    quad_c, quad_m, shift_c, shift_m, res_c, res_m, rim_c, rim_m,
    amp_v, parts, part_y, part_x,
    load, sem_cs, sem_cr, sem_ms, sem_mr, sem_fs, sem_fr, sem_bs, sem_br,
    a2a_s, a2a_r, sem_ts, sem_tr, sem_ys, sem_yr, sem_xs, sem_xr,
):
    gx, gy = lax.axis_index("gx"), lax.axis_index("gy")
    at = (gx, gy, m, n)
    nc, nm, nf = xi_c.shape[0], xi_m.shape[0], xi_f.shape[0]
    slab = nf // n
    facets = k_u.shape[1]
    bins = v_d.shape[2]

    loads = [
        pltpu.make_async_copy(src, dst, load.at[i])
        for i, (src, dst) in enumerate(
            (
                (xi_c, pad_c.at[ROW : ROW + nc, LANE : LANE + nc]),
                (co_m, cm),
                (xi_m, xm),
                (co_f, cf),
                (xi_f, xf),
                (k_u.at[0], ku),
                (k_v.at[0], kv),
                (v_d.at[0], vd),
            )
        )
    ]
    for c in loads:
        c.start()

    barrier = pltpu.get_barrier_semaphore()
    greeted = 0
    for k in range(1, n):
        pl.semaphore_signal(barrier, inc=1, device_id=(gx, lax.rem(gy + k, n)), device_id_type=MESH)
        greeted += 1
    for k in range(1, m):
        pl.semaphore_signal(barrier, inc=1, device_id=(lax.rem(gx + k, m), gy), device_id_type=MESH)
        greeted += 1
    for dx in (-1, 1):
        for dy in (-1, 1):
            pl.semaphore_signal(
                barrier, inc=1, device_id=(lax.rem(gx + dx + m, m), lax.rem(gy + dy + n, n)), device_id_type=MESH
            )
            greeted += 1
    loads[0].wait()
    pl.semaphore_wait(barrier, greeted)

    halo_c = Halo(pad_c, pad_c, nc, nc, True, sem_cs, sem_cr, at)
    halo_c.start()

    def meta_copy(k):
        return pltpu.make_async_remote_copy(
            src_ref=meta,
            dst_ref=metas.at[gy],
            send_sem=sem_ts.at[k],
            recv_sem=sem_tr.at[k],
            device_id=(gx, lax.rem(gy + k, n)),
            device_id_type=MESH,
        )

    @pl.loop(1, n)
    def _(k):
        meta_copy(k).start()

    metas[gy] = meta[...]
    spread(mat_c)
    spread(mat_m)

    loads[1].wait()
    loads[2].wait()
    halo_c.wait()
    refine(pad_c, win_c, cm, roll_c, hi_c, lo_c, nc, 32)
    interleave(hi_c, lo_c, mat_c, lace_c, nc)
    for c in range(nm // LANE):
        cols = slice(c * LANE, (c + 1) * LANE)
        pad_m[ROW : ROW + nm, LANE + c * LANE : LANE + (c + 1) * LANE] = lace_c[c] + xm[:, cols]
    halo_m = Halo(pad_m, pad_m, nm, nm, True, sem_ms, sem_mr, at)
    halo_m.start()

    @pl.loop(1, n)
    def _(k):
        meta_copy(k).wait()

    lane = lax.broadcasted_iota(jnp.int32, (slab, nf), 1)
    row = lax.broadcasted_iota(jnp.int32, (slab, nf), 0)
    tile_of = (lane // slab).astype(jnp.float32)
    same = lane % slab == row

    @pl.loop(0, n)
    def _(o):
        rows = pl.ds(pl.multiple_of(o * slab, slab), slab)
        value = metas[o]
        for f in range(facets):
            total = jnp.zeros((slab, nf), jnp.float32)
            for s in range(2):
                i = 2 * f + s
                tile = jnp.concatenate([value[i : i + 1, :]] * (nf // LANE), axis=1)
                weight = jnp.concatenate([value[4 + i : 5 + i, :]] * (nf // LANE), axis=1)
                total = total + jnp.where((tile == tile_of) & same, weight, 0.0)
            mix_hi[f, rows, :], mix_lo[f, rows, :] = split(total)

    loads[3].wait()
    loads[4].wait()
    halo_m.wait()
    refine(pad_m, win_m, cf, roll_m, hi_m, lo_m, nm, 16)
    interleave(hi_m, lo_m, mat_m, lace_m, nm)
    for c in range(nf // LANE):
        cols = slice(c * LANE, (c + 1) * LANE)
        sky[:, cols] = (lace_m[c] + xf[:, cols]).astype(jnp.bfloat16)

    def exchange(i, src, dst):
        return Exchange(src, dst, a2a_s.at[i], a2a_r.at[i], at, slab)

    first = exchange(0, sky, tiles)
    first.start()
    prior = fold_lanes(squares(pad_c[ROW : ROW + nc, LANE : LANE + nc]))
    prior = prior + fold_lanes(squares(xm[...])) + fold_lanes(squares(xf[...]))
    parts[...] = jnp.zeros_like(parts)
    first.wait()
    out = []
    for f in range(facets):
        sums[f] = (f32dot(mix_hi[f], tiles[...], (1, 0)) + f32dot(mix_lo[f], tiles[...], (1, 0))).astype(jnp.bfloat16)
        out.append(exchange(1 + f, sums.at[f], fsum.at[f]))
        out[f].start()

    loads[5].wait()
    loads[6].wait()
    loads[7].wait()
    home = []
    chunk = 256
    for f in range(facets):
        out[f].wait()
        count = counts[0, f]
        amp_v[...] = jnp.zeros_like(amp_v)

        @pl.loop(0, bins // chunk)
        def _(step):
            here = pl.ds(pl.multiple_of(step * chunk, chunk), chunk)
            u = ku[f, here, :]
            amp = f32dot(u, fsum[f], (1, 0)).astype(jnp.bfloat16)
            vis = f32dot(amp, kv[f], (1, 1))
            bin_at = step * chunk + lax.broadcasted_iota(jnp.int32, (chunk, bins), 0)
            resid = jnp.where(bin_at < count, vis - vd[f, here, :].astype(jnp.float32), 0.0)
            parts[...] += squares(resid)
            dvis = (inv_noise * resid).astype(jnp.bfloat16)
            damp = f32dot(dvis, kv[f], (1, 0)).astype(jnp.bfloat16)
            amp_v[...] += f32dot(u, damp, (0, 0))

        dsum[f] = amp_v[...].astype(jnp.bfloat16)
        home.append(exchange(1 + facets + f, dsum.at[f], dslab.at[f]))
        home[f].start()

    own = 0.5 * prior + 0.5 * inv_noise * fold_lanes(parts[...])
    part_y[gy] = jnp.where(lax.broadcasted_iota(jnp.int32, (ROW, LANE), 0) == 0, own, 0.0)

    def pot_y(k):
        return pltpu.make_async_remote_copy(
            src_ref=part_y.at[gy],
            dst_ref=part_y.at[gy],
            send_sem=sem_ys.at[k],
            recv_sem=sem_yr.at[k],
            device_id=(gx, lax.rem(gy + k, n)),
            device_id_type=MESH,
        )

    def pot_x(k):
        return pltpu.make_async_remote_copy(
            src_ref=part_x.at[gx],
            dst_ref=part_x.at[gx],
            send_sem=sem_xs.at[k],
            recv_sem=sem_xr.at[k],
            device_id=(lax.rem(gx + k, m), gy),
            device_id_type=MESH,
        )

    @pl.loop(1, n)
    def _(k):
        pot_y(k).start()

    for f in range(facets):
        home[f].wait()
        part = f32dot(mix_hi[f], dslab[f], (0, 0)) + f32dot(mix_lo[f], dslab[f], (0, 0))
        if f == 0:
            amp_v[...] = part
        else:
            amp_v[...] += part
    back_b[...] = amp_v[...].astype(jnp.bfloat16)
    last = exchange(1 + 2 * facets, back_b, dsky)
    last.start()

    @pl.loop(1, n)
    def _(k):
        pot_y(k).wait()

    part_x[gx] = jnp.sum(part_y[...], axis=0)

    @pl.loop(1, m)
    def _(k):
        pot_x(k).start()

    last.wait()
    for a in (0, 1):
        rows = slice(a * nm, (a + 1) * nm)
        lined = f32dot(mat_m[rows, :], dsky[...], (1, 0)).astype(jnp.bfloat16)
        quad_m[rows, :] = f32dot(lined, mat_m[...], (1, 1))
    parent_terms(quad_m, cf, shift_m, res_m, nm, 16)
    halo_f = Halo(res_m, rim_m, nm, nm, False, sem_fs, sem_fr, at)
    halo_f.start()
    g_f[...] = dsky[...].astype(jnp.float32) + xf[...]
    halo_f.wait()
    fold_rim(res_m, rim_m, nm)
    dmiddle = res_m[ROW : ROW + nm, LANE : LANE + nm]
    g_m[...] = dmiddle + xm[...]
    high, low = split(dmiddle)
    for a in (0, 1):
        rows = slice(a * nc, (a + 1) * nc)
        matrix = mat_c[rows, :]
        quad_c[rows, :] = f32dot(
            f32dot(matrix, high, (1, 0)).astype(jnp.bfloat16), mat_c[...], (1, 1)
        ) + f32dot(f32dot(matrix, low, (1, 0)).astype(jnp.bfloat16), mat_c[...], (1, 1))
    parent_terms(quad_c, cm, shift_c, res_c, nc, 32)
    halo_b = Halo(res_c, rim_c, nc, nc, False, sem_bs, sem_br, at)
    halo_b.start()

    @pl.loop(1, m)
    def _(k):
        pot_x(k).wait()

    pot[0, 0] = jnp.sum(part_x[...]) / cells
    halo_b.wait()
    fold_rim(res_c, rim_c, nc)
    g_c[...] = res_c[ROW : ROW + nc, LANE : LANE + nc] + pad_c[ROW : ROW + nc, LANE : LANE + nc]


def body(
    xi_coarse, xi_middle, xi_fine, coef_middle, coef_fine, kern_u, kern_v, vis_data, facet_tiles, facet_weight, facet_count
):
    m, n = lax.axis_size("gx"), lax.axis_size("gy")
    nc, nm, nf = xi_coarse.shape[0], xi_middle.shape[0], xi_fine.shape[0]
    facets, bins = kern_u.shape[1], vis_data.shape[2]
    cells = float(m * n * nf * nf)
    meta = jnp.concatenate([facet_tiles.reshape(4).astype(jnp.float32), facet_weight.reshape(4)])
    meta = jnp.broadcast_to(meta[:, None], (8, LANE))
    f32, bf16 = jnp.float32, jnp.bfloat16
    vmem, dma = pltpu.VMEM, pltpu.SemaphoreType.DMA

    def wide(size):
        return vmem((size + 2 * ROW, size + 2 * LANE), f32)

    scratch = [
        wide(nc), wide(nm), vmem((nm, nm), f32), vmem((nf, nf), f32),
        vmem(coef_middle.shape, bf16), vmem(coef_fine.shape, bf16),
        vmem(kern_u.shape[1:], bf16), vmem(kern_v.shape[1:], bf16), vmem(vis_data.shape[1:], bf16),
        vmem((nc + 2 * ROW, nc), f32), vmem((nm + 2 * ROW, nm), f32),
        vmem((9, nc, nc), f32), vmem((9, nm, nm), f32),
        vmem((nm, nm), bf16), vmem((nm, nm), bf16), vmem((nf, nf), bf16), vmem((nf, nf), bf16),
        vmem((nm // LANE, nm, LANE), f32), vmem((nf // LANE, nf, LANE), f32),
        vmem((nm, nm), bf16), vmem((nf, nf), bf16),
        vmem((n, 8, LANE), f32), vmem((facets, nf, nf), bf16), vmem((facets, nf, nf), bf16),
        vmem((nf, nf), bf16), vmem((nf, nf), bf16),
        vmem((facets, nf, nf), bf16), vmem((facets, nf, nf), bf16),
        vmem((facets, nf, nf), bf16), vmem((facets, nf, nf), bf16),
        vmem((nf, nf), bf16), vmem((nf, nf), bf16),
        vmem((nm, nm), f32), vmem((nf, nf), f32),
        vmem((3, nc + 4 * ROW, nc + 2 * LANE), f32), vmem((3, nm + 4 * ROW, nm + 2 * LANE), f32),
        wide(nc), wide(nm), wide(nc), wide(nm),
        vmem((nf, nf), f32), vmem((1, bins), f32), vmem((n, 8, LANE), f32), vmem((m, 8, LANE), f32),
        dma((8,)),
        *[dma((8,)) for _ in range(8)],
        dma((2 + 2 * facets, n)), dma((2 + 2 * facets, n)),
        dma((n,)), dma((n,)), dma((n,)), dma((n,)), dma((m,)), dma((m,)),
    ]
    hbm = pl.BlockSpec(memory_space=pl.ANY)
    here = pl.BlockSpec(memory_space=pltpu.VMEM)
    small = pl.BlockSpec(memory_space=pltpu.SMEM)
    grads = pl.pallas_call(
        functools.partial(kernel, m, n, cells),
        name="prior_gradient",
        out_shape=(
            jax.ShapeDtypeStruct(xi_coarse.shape, f32),
            jax.ShapeDtypeStruct(xi_middle.shape, f32),
            jax.ShapeDtypeStruct(xi_fine.shape, f32),
            jax.ShapeDtypeStruct((1, 1), f32),
        ),
        in_specs=[hbm] * 8 + [here, small],
        out_specs=(here, here, here, small),
        scratch_shapes=scratch,
        compiler_params=pltpu.CompilerParams(
            collective_id=0, has_side_effects=True, vmem_limit_bytes=60 * 1024 * 1024
        ),
    )(xi_coarse, xi_middle, xi_fine, coef_middle, coef_fine, kern_u, kern_v, vis_data, meta, facet_count)
    return (*grads[:3], grads[3].reshape(()))


def solution(mesh):
    placed = (
        P("gx", "gy"),
        P("gx", "gy"),
        P("gx", "gy"),
        P(None, None, "gx", "gy"),
        P(None, None, "gx", "gy"),
        P("gx", "gy", None, None),
        P("gx", "gy", None, None),
        P("gx", "gy", None, None),
        P("gx", "gy", None),
        P("gx", "gy", None),
        P("gx", "gy"),
    )
    return jax.shard_map(
        body,
        mesh=mesh,
        in_specs=placed,
        out_specs=(P("gx", "gy"), P("gx", "gy"), P("gx", "gy"), P()),
        check_vma=False,
    )
```

time: 693 us -> 99.8 us (0.14); the launches traced: 684 us -> 99.5 us
  local copies, waits for them, and re-layouts: 265 us -> 6.91 us
  waiting for transfers between devices: 174 us -> 0 us
  blocking collectives: 111 us -> 0 us
  Pallas kernels: 0 us -> 89.5 us
  other arithmetic: 58 us -> 0.76 us
  starting transfers between devices: 38.5 us -> 0 us
  matrix products: 18.2 us -> 0 us
  between operations: 19.3 us -> 2.41 us
    reshape x5 -> x1, local copies, waits for them, and re-layouts: 169 us -> 0.76 us  [body(): facet_weight.reshape(4)]
    all_gather x2 -> x0, waiting for transfers between devices: 148 us -> none  [the longest x1 83.7 us: body(): piece = lax.all_gather(sky_tile, 'gy', axis=1, tiled=True)]
    pallas_call x0 -> x1, Pallas kernels: none -> 89.5 us  [body(): pl.pallas_call(functools.partial(kernel, m, n, cells), name='prior_gradie...]
    psum x1 -> x0, blocking collectives: 69.4 us -> none  [body(): total = lax.psum(prior + likelihood, ('gx', 'gy'))]
    transpose x2 -> x0, local copies, waits for them, and re-layouts: 46.8 us -> none  [back(): grad.reshape(rows, 2, cols, 2).transpose(1, 3, 0, 2).reshape(4, rows, cols)]
    all_gather x2 -> x0, blocking collectives: 41.8 us -> none  [the longest x1 21.8 us: body(): piece_list = lax.all_gather(facet_tiles, 'gy', axis=1, tiled=True)]
    ppermute x16 -> x0, starting transfers between devices: 38.2 us -> none  [the longest x8 27.9 us: extended(): before = lax.ppermute(last, axis, up)]
    reduce_sum x7 -> x0, other arithmetic: 28 us -> none  [the longest x1 15.8 us: body(): sums = jnp.sum(mixing[:, None, :, None] * blocks[None], axis=2)]
  transfers between devices with their start and end apart: 18 -> 0, of which waited for: 10 -> 0; matrix products, arithmetic and copies ran while one was open for 1% -> 0% of each run, Pallas kernels for 0% -> 0%
where the time goes in v1:
time: 99.8 us; the launch traced here: 99.5 us
  Pallas kernels  89.5 us (90%)
  local copies, waits for them, and re-layouts  6.91 us (7%)
  between operations  2.41 us (2%)
    pallas_call x1, Pallas kernels, body(): pl.pallas_call(functools.partial(kernel, m, n, cells), name='prior_gradie...  89.5 us
    unnamed x3, local copies, waits for them, and re-layouts  5.4 us

profile of v1, /device:TPU:0, one launch (start us, length us, event | category | flops | bytes accessed | tf_op | source)
XLA Modules:
  0.0 99.5 jit_solution(5099487684136252125)
XLA Ops:
  0.6 0.8 reshape.17
  1.4 0.7 convert_element_type.6
  2.1 0.1 convert_element_type.7
  2.2 0.1 pad_maximum_fusion
  2.2 0.7 broadcast_in_dim.2.meta
  2.9 89.5 %prior_gradient.1 = (f32[128,128]{1,0:T(8,128)}, f32[256,256]{1,0:T(8,128)}, f32[512,512]{1,0:T(8,128)}, f32[1,1]{1,0:T(1,128)}) custom-call(f32[128,128]{1,0:T(8,128)} %xi_c.1, f32[256,256]{1,0:T(8,128)} %xi_m.1, f32[512,512]{1,0:T(8,128)} %xi_f.1, bf16[4,9,128,128]{3,2,1,0:T(8,128)(2,1)} %co_m.1, bf16[4,9,256,256]{3,2,1,0:T(8,128)(2,1)} %co_f.1, ...), custom_call_target="tpu_custom_call" | custom-call | tf_op jit(solution)/shard_map/prior_gradient/pallas_call | solution.py:492
  92.4 1.5 %copy.19 = f32[128,128]{1,0:T(8,128)} copy(f32[128,128]{1,0:T(8,128)} %get-tuple-element.16) | data formatting | bytes 131072
  93.8 1.7 %copy.20 = f32[256,256]{1,0:T(8,128)} copy(f32[256,256]{1,0:T(8,128)} %get-tuple-element.17) | data formatting | bytes 524288
  95.5 2.3 %copy.21 = f32[512,512]{1,0:T(8,128)} copy(f32[512,512]{1,0:T(8,128)} %get-tuple-element.18) | data formatting | bytes 2097152

commit v2 on v1

v2 whole, which is shorter than its diff:
```python
import functools

import jax
import jax.numpy as jnp
from jax import lax
from jax.experimental import pallas as pl
from jax.experimental.pallas import tpu as pltpu
from jax.sharding import PartitionSpec as P

inv_noise = 0.125
MESH = pl.DeviceIdType.MESH
ROW, LANE = 8, 128
SIDES = [(dx, dy) for dx in (-1, 0, 1) for dy in (-1, 0, 1) if (dx, dy) != (0, 0)]


def f32dot(a, b, contract):
    return lax.dot_general(a, b, ((contract[:1], contract[1:]), ((), ())), preferred_element_type=jnp.float32)


def split(x):
    high = x.astype(jnp.bfloat16)
    return high, (x - high.astype(jnp.float32)).astype(jnp.bfloat16)


def strip(side, size, edge, near):
    if side == 0:
        return edge, size
    if near:
        return (edge, edge) if side < 0 else (size, edge)
    return (0, edge) if side < 0 else (edge + size, edge)


def diagonal():
    row = lax.broadcasted_iota(jnp.int32, (LANE, LANE), 0)
    return row == lax.broadcasted_iota(jnp.int32, (LANE, LANE), 1)


class Halo:
    def __init__(self, src, rows_in, cols_out, cols_in, near, send, recv, at):
        gx, gy, m, n = at
        self.src, self.rows_in, self.cols_out, self.cols_in, self.near, self.at = src, rows_in, cols_out, cols_in, near, at
        self.size = size = src.shape[0] - 2 * ROW
        self.copies = []
        for i, (dx, dy) in enumerate(SIDES):
            side = 0 if max(dx, -1) > 0 or (dx == 0 and dy > 0) else 1
            if dx:
                source = src.at[pl.ds(*strip(dx, size, ROW, near)), pl.ds(*strip(dy, size, LANE, near))]
                target = rows_in.at[side, :, pl.ds(*strip(-dy, size, LANE, False))]
            else:
                source, target = cols_out.at[side], cols_in.at[side]
            self.copies.append(
                pltpu.make_async_remote_copy(
                    src_ref=source,
                    dst_ref=target,
                    send_sem=send.at[i],
                    recv_sem=recv.at[i],
                    device_id=(lax.rem(gx + dx + m, m), lax.rem(gy + dy + n, n)),
                    device_id_type=MESH,
                )
            )

    def start(self):
        size, eye = self.size, diagonal()
        for side, dy in ((0, 1), (1, -1)):
            lane = (LANE + size - 1 if dy > 0 else LANE) if self.near else (LANE + size if dy > 0 else LANE - 1)
            tile = lane // LANE * LANE
            for b in range(size // LANE):
                block = self.src[ROW + b * LANE : ROW + (b + 1) * LANE, tile : tile + LANE]
                block = jnp.broadcast_to(block[:, lane - tile : lane - tile + 1], (LANE, LANE))
                self.cols_out[side, b : b + 1, :] = jnp.sum(jnp.where(eye, block, 0.0), axis=0, keepdims=True)
        for c in self.copies:
            c.start()

    def wait(self):
        for c in self.copies:
            c.wait()

    def column(self, side):
        gx, gy, m, n = self.at
        inside = gy > 0 if side == 0 else gy < n - 1
        blocks = []
        for b in range(self.size // LANE):
            block = jnp.broadcast_to(self.cols_in[side, b : b + 1, :], (LANE, LANE))
            blocks.append(jnp.sum(jnp.where(diagonal(), block, 0.0), axis=1, keepdims=True))
        return jnp.where(inside, jnp.concatenate(blocks, axis=0), 0.0)

    def strips(self, side):
        gx, gy, m, n = self.at
        inside = gx > 0 if side == 0 else gx < m - 1
        value = jnp.where(inside, self.rows_in[side], 0.0)
        left, right = value[:, 0:LANE], value[:, LANE + self.size : 2 * LANE + self.size]
        return jnp.where(gy > 0, left, 0.0), value[:, LANE : LANE + self.size], jnp.where(gy < n - 1, right, 0.0)

    def surround(self, pad):
        size = self.size
        for side, start in ((0, 0), (1, ROW + size)):
            pad[start : start + ROW, :] = jnp.concatenate(self.strips(side), axis=1)
        for side, start in ((0, 0), (1, LANE + size)):
            pad[ROW : ROW + size, start : start + LANE] = jnp.broadcast_to(self.column(side), (size, LANE))

    def fold(self, result):
        size = self.size
        first, last = slice(LANE, 2 * LANE), slice(size, size + LANE)
        for side, rows in ((0, slice(ROW, 2 * ROW)), (1, slice(size, size + ROW))):
            left, middle, right = self.strips(side)
            result[rows, LANE : LANE + size] += middle
            result[rows, first] += left
            result[rows, last] += right
        lane = lax.broadcasted_iota(jnp.int32, (size, LANE), 1)
        full = slice(ROW, ROW + size)
        result[full, first] += jnp.where(lane == 0, self.column(0), 0.0)
        result[full, last] += jnp.where(lane == LANE - 1, self.column(1), 0.0)


class Exchange:
    def __init__(self, src, dst, send, recv, at, slab, cols=None):
        self.src, self.dst, self.send, self.recv, self.at, self.slab = src, dst, send, recv, at, slab
        self.cols = slice(0, src.shape[1]) if cols is None else cols

    def rows(self, index):
        return pl.ds(pl.multiple_of(index * self.slab, self.slab), self.slab)

    def copy(self, k):
        gx, gy, m, n = self.at
        peer = lax.rem(gy + k, n)
        return pltpu.make_async_remote_copy(
            src_ref=self.src.at[self.rows(peer), self.cols],
            dst_ref=self.dst.at[self.rows(gy), self.cols],
            send_sem=self.send.at[k],
            recv_sem=self.recv.at[k],
            device_id=(gx, peer),
            device_id_type=MESH,
        )

    def own(self):
        here = self.rows(self.at[1])
        self.dst[here, self.cols] = self.src[here, self.cols]

    def start(self):
        @pl.loop(1, self.at[3])
        def _(k):
            self.copy(k).start()

        self.own()

    def wait(self):
        @pl.loop(1, self.at[3])
        def _(k):
            self.copy(k).wait()

    def meets(self, index, ends):
        n = self.at[3]
        at_end = (index == 0) | (index == n - 1)
        return at_end if ends else jnp.logical_not(at_end)

    def start_some(self, low, high, ends):
        gx, gy, m, n = self.at

        @pl.loop(low, high)
        def _(k):
            @pl.when(self.meets(lax.rem(gy + k, n), ends))
            def _():
                self.copy(k).start()

    def wait_some(self, ends):
        gx, gy, m, n = self.at

        @pl.loop(1, n)
        def _(k):
            @pl.when(self.meets(lax.rem(gy + k, n), ends))
            def _():
                self.copy(k).wait_send()

        @pl.when(self.meets(gy, ends))
        def _():
            @pl.loop(1, n)
            def _(k):
                self.copy(k).wait_recv()


def spread(ref):
    size = ref.shape[0]
    half = size // 2
    row = lax.broadcasted_iota(jnp.int32, (half, size), 0)
    col = lax.broadcasted_iota(jnp.int32, (half, size), 1)
    ref[0:half, :] = jnp.where(col == 2 * row, 1.0, 0.0).astype(jnp.bfloat16)
    ref[half:size, :] = jnp.where(col == 2 * row + 1, 1.0, 0.0).astype(jnp.bfloat16)


def refine(pad, wins, coef, rolled, high, low, size, rows):
    width = size + 2 * LANE
    for dj in (-1, 0, 1):
        value = pad[...]
        if dj:
            value = pltpu.roll(value, (-dj) % width, 1)
        rolled[...] = value[:, LANE : LANE + size]
        for di in (-1, 0, 1):
            wins[3 * (di + 1) + dj + 1] = rolled[ROW + di : ROW + di + size, :]

    @pl.loop(0, size // rows)
    def _(step):
        at = pl.multiple_of(step * rows, rows)
        here = pl.ds(at, rows)
        totals = [None] * 4
        for near in range(9):
            window = wins[near, here, :]
            for child in range(4):
                term = coef[child, near, here, :].astype(jnp.float32) * window
                totals[child] = term if near == 0 else totals[child] + term
        for child in range(4):
            a, b = child // 2, child % 2
            there = pl.ds(pl.multiple_of(a * size + at, rows), rows)
            high[there, b * size : (b + 1) * size], low[there, b * size : (b + 1) * size] = split(totals[child])


def interleave(high, low, matrix, laced, size):
    for a in (0, 1):
        rows = slice(a * size, (a + 1) * size)
        value = f32dot(high[rows, :], matrix[...], (1, 0)) + f32dot(low[rows, :], matrix[...], (1, 0))
        for c in range(2 * size // LANE):
            laced[c, pl.ds(a, size, stride=2), :] = value[:, c * LANE : (c + 1) * LANE]


def parent_terms(quads, coef, shifted, result, size, rows):
    width = size + 2 * LANE
    tall = size + 4 * ROW
    for d in range(3):
        shifted[d, 0 : 2 * ROW, :] = jnp.zeros((2 * ROW, width), jnp.float32)
        shifted[d, tall - 2 * ROW : tall, :] = jnp.zeros((2 * ROW, width), jnp.float32)

    @pl.loop(0, size // rows)
    def _(step):
        at = pl.multiple_of(step * rows, rows)
        here = pl.ds(at, rows)
        quad = [
            quads[pl.ds(pl.multiple_of(a * size + at, rows), rows), b * size : (b + 1) * size]
            for a in (0, 1)
            for b in (0, 1)
        ]
        blank = jnp.zeros((rows, LANE), jnp.float32)
        for d in range(3):
            total = None
            for j in range(3):
                part = None
                for child in range(4):
                    term = coef[child, 3 * d + j, here, :].astype(jnp.float32) * quad[child]
                    part = term if child == 0 else part + term
                part = jnp.concatenate([blank, part, blank], axis=1)
                if j != 1:
                    part = pltpu.roll(part, (j - 1) % width, 1)
                total = part if j == 0 else total + part
            shifted[d, pl.ds(pl.multiple_of(at + 2 * ROW, ROW), rows), :] = total

    high = tall - 2 * ROW
    result[...] = (
        shifted[1, ROW : ROW + high, :]
        + shifted[2, ROW - 1 : ROW - 1 + high, :]
        + shifted[0, ROW + 1 : ROW + 1 + high, :]
    )


def squares(x):
    return jnp.sum(x * x, axis=0, keepdims=True)


def fold_lanes(x):
    total = x[:, 0:LANE]
    for c in range(1, x.shape[1] // LANE):
        total = total + x[:, c * LANE : (c + 1) * LANE]
    return total


def kernel(
    m, n, cells,
    xi_c, xi_m, xi_f, co_m, co_f, k_u, k_v, v_d, listed, weights, counts,
    g_c, g_m, g_f, pot,
    pad_c, pad_m, xm, xf, cm, cf, ku, kv, vd, kut,
    roll_c, roll_m, win_c, win_m, hi_c, lo_c, hi_m, lo_m, lace_c, lace_m, mat_c, mat_m,
    meta, metas, mix_hi, mix_lo, sky, sky_2, edge, edges, tiles, sums, fsum, damps, dsum, dslab, back_b, dsky,
    quad_c, quad_m, shift_c, shift_m, res_c, res_m, grad_c, grad_m, grad_f, back_v,
    row_c, row_m, row_f, row_b, col_o, col_i,
    parts, part_y, part_x,
    load, save, sem_s, sem_r, a2a_s, a2a_r, sem_ts, sem_tr, sem_ys, sem_yr, sem_xs, sem_xr,
):
    gx, gy = lax.axis_index("gx"), lax.axis_index("gy")
    at = (gx, gy, m, n)
    nc, nm, nf = xi_c.shape[0], xi_m.shape[0], xi_f.shape[0]
    slab = nf // n
    facets = k_u.shape[1]
    bins = v_d.shape[2]

    barrier = pltpu.get_barrier_semaphore()
    greeted = 0
    for dx in (-1, 1):
        for dy in (-1, 1):
            pl.semaphore_signal(
                barrier, inc=1, device_id=(lax.rem(gx + dx + m, m), lax.rem(gy + dy + n, n)), device_id_type=MESH
            )
            greeted += 1
    for k in range(1, m):
        pl.semaphore_signal(barrier, inc=1, device_id=(lax.rem(gx + k, m), gy), device_id_type=MESH)
        greeted += 1
    for k in range(1, n):
        pl.semaphore_signal(barrier, inc=1, device_id=(gx, lax.rem(gy + k, n)), device_id_type=MESH)
        greeted += 1

    loads = [
        pltpu.make_async_copy(src, dst, load.at[i])
        for i, (src, dst) in enumerate(
            (
                (xi_c, pad_c.at[ROW : ROW + nc, LANE : LANE + nc]),
                (co_m, cm),
                (xi_m, xm),
                (co_f, cf),
                (xi_f, xf),
                (k_u.at[0], ku),
                (k_v.at[0], kv),
                (v_d.at[0], vd),
            )
        )
    ]
    for c in loads:
        c.start()

    def blank(pad, size):
        width = size + 2 * LANE
        pad[0:ROW, :] = jnp.zeros((ROW, width), jnp.float32)
        pad[ROW + size : 2 * ROW + size, :] = jnp.zeros((ROW, width), jnp.float32)
        pad[ROW : ROW + size, 0:LANE] = jnp.zeros((size, LANE), jnp.float32)
        pad[ROW : ROW + size, LANE + size : width] = jnp.zeros((size, LANE), jnp.float32)

    def middle_level():
        refine(pad_c, win_c, cm, roll_c, hi_c, lo_c, nc, 32)
        interleave(hi_c, lo_c, mat_c, lace_c, nc)
        for c in range(nm // LANE):
            cols = slice(c * LANE, (c + 1) * LANE)
            pad_m[ROW : ROW + nm, LANE + c * LANE : LANE + (c + 1) * LANE] = lace_c[c] + xm[:, cols]

    def fine_level(out):
        refine(pad_m, win_m, cf, roll_m, hi_m, lo_m, nm, 16)
        interleave(hi_m, lo_m, mat_m, lace_m, nm)
        for c in range(nf // LANE):
            cols = slice(c * LANE, (c + 1) * LANE)
            out[:, cols] = (lace_m[c] + xf[:, cols]).astype(jnp.bfloat16)

    def halo(i, src, rows_in, near):
        return Halo(src, rows_in, col_o.at[i], col_i.at[i], near, sem_s.at[i], sem_r.at[i], at)

    def exchange(i, src, dst, cols=None):
        return Exchange(src, dst, a2a_s.at[i], a2a_r.at[i], at, slab, cols)

    spread(mat_c)
    spread(mat_m)
    blank(pad_c, nc)
    blank(pad_m, nm)
    for f in range(facets):
        for s in range(2):
            i = 2 * f + s
            meta[i : i + 1, :] = jnp.full((1, LANE), listed[0, f, s].astype(jnp.float32))
            meta[4 + i : 5 + i, :] = jnp.full((1, LANE), weights[0, f, s])
    for c in loads[:3]:
        c.wait()
    middle_level()
    col_o[...] = jnp.zeros_like(col_o)
    pl.semaphore_wait(barrier, greeted)

    halo_c = halo(0, pad_c, row_c, True)
    halo_c.start()

    def meta_copy(k):
        return pltpu.make_async_remote_copy(
            src_ref=meta,
            dst_ref=metas.at[gy],
            send_sem=sem_ts.at[k],
            recv_sem=sem_tr.at[k],
            device_id=(gx, lax.rem(gy + k, n)),
            device_id_type=MESH,
        )

    @pl.loop(1, n)
    def _(k):
        meta_copy(k).start()

    metas[gy] = meta[...]
    for c in loads[3:5]:
        c.wait()
    fine_level(sky)
    early = exchange(0, sky, tiles)
    early.start_some(1, n // 2, False)

    halo_c.wait()
    halo_c.surround(pad_c)
    middle_level()
    halo_m = halo(1, pad_m, row_m, True)
    halo_m.start()
    early.start_some(n // 2, n, False)

    @pl.loop(1, n)
    def _(k):
        meta_copy(k).wait()

    lane = lax.broadcasted_iota(jnp.int32, (slab, nf), 1)
    row = lax.broadcasted_iota(jnp.int32, (slab, nf), 0)
    tile_of = (lane // slab).astype(jnp.float32)
    same = lane % slab == row

    @pl.loop(0, n)
    def _(o):
        rows = pl.ds(pl.multiple_of(o * slab, slab), slab)
        value = metas[o]
        for f in range(facets):
            total = jnp.zeros((slab, nf), jnp.float32)
            for s in range(2):
                i = 2 * f + s
                tile = jnp.concatenate([value[i : i + 1, :]] * (nf // LANE), axis=1)
                weight = jnp.concatenate([value[4 + i : 5 + i, :]] * (nf // LANE), axis=1)
                total = total + jnp.where((tile == tile_of) & same, weight, 0.0)
            mix_hi[f, rows, :], mix_lo[f, rows, :] = split(total)

    halo_m.wait()
    halo_m.surround(pad_m)
    fine_level(sky_2)
    left, right = slice(0, LANE), slice(nf - LANE, nf)
    outer = lax.broadcasted_iota(jnp.int32, (nf, LANE), 1) < LANE // 2
    edge[...] = jnp.where(outer, sky_2[:, left], sky_2[:, right])
    late = exchange(1, sky_2, tiles)
    rim = exchange(2, edge, edges)
    late.start_some(1, n, True)
    rim.start()
    late.own()
    prior = fold_lanes(squares(pad_c[ROW : ROW + nc, LANE : LANE + nc]))
    prior = prior + fold_lanes(squares(xm[...])) + fold_lanes(squares(xf[...]))
    parts[...] = jnp.zeros_like(parts)
    early.wait_some(False)
    late.wait_some(True)
    rim.wait()
    tiles[:, left] = jnp.where(outer, edges[...], tiles[:, left])
    tiles[:, right] = jnp.where(outer, tiles[:, right], edges[...])
    out = []
    for f in range(facets):
        sums[f] = (f32dot(mix_hi[f], tiles[...], (1, 0)) + f32dot(mix_lo[f], tiles[...], (1, 0))).astype(jnp.bfloat16)
        out.append(exchange(3 + f, sums.at[f], fsum.at[f]))
        out[f].start()

    for c in loads[5:]:
        c.wait()
    for f in range(facets):
        kut[f] = ku[f].T
    home = []
    chunk = 256
    halves = [slice(h * nf // 2, (h + 1) * nf // 2) for h in (0, 1)]
    for f in range(facets):
        out[f].wait()
        count = counts[0, f]

        @pl.loop(0, bins // chunk)
        def _(step):
            here = pl.ds(pl.multiple_of(step * chunk, chunk), chunk)
            amp = f32dot(ku[f, here, :], fsum[f], (1, 0)).astype(jnp.bfloat16)
            vis = f32dot(amp, kv[f], (1, 1))
            bin_at = step * chunk + lax.broadcasted_iota(jnp.int32, (chunk, bins), 0)
            resid = jnp.where(bin_at < count, vis - vd[f, here, :].astype(jnp.float32), 0.0)
            parts[...] += squares(resid)
            dvis = (inv_noise * resid).astype(jnp.bfloat16)
            damps[here, :] = f32dot(dvis, kv[f], (1, 0)).astype(jnp.bfloat16)

        for h, cols in enumerate(halves):
            dsum[f, :, cols] = f32dot(kut[f], damps[:, cols], (1, 0)).astype(jnp.bfloat16)
            home.append(exchange(3 + facets + 2 * f + h, dsum.at[f], dslab.at[f], cols))
            home[-1].start()

    own = 0.5 * prior + 0.5 * inv_noise * fold_lanes(parts[...])
    part_y[gy] = jnp.where(lax.broadcasted_iota(jnp.int32, (ROW, LANE), 0) == 0, own, 0.0)

    def pot_y(k):
        return pltpu.make_async_remote_copy(
            src_ref=part_y.at[gy],
            dst_ref=part_y.at[gy],
            send_sem=sem_ys.at[k],
            recv_sem=sem_yr.at[k],
            device_id=(gx, lax.rem(gy + k, n)),
            device_id_type=MESH,
        )

    def pot_x(k):
        return pltpu.make_async_remote_copy(
            src_ref=part_x.at[gx],
            dst_ref=part_x.at[gx],
            send_sem=sem_xs.at[k],
            recv_sem=sem_xr.at[k],
            device_id=(lax.rem(gx + k, m), gy),
            device_id_type=MESH,
        )

    @pl.loop(1, n)
    def _(k):
        pot_y(k).start()

    def unmix(f, cols):
        return f32dot(mix_hi[f], dslab[f, :, cols], (0, 0)) + f32dot(mix_lo[f], dslab[f, :, cols], (0, 0))

    for f in range(facets - 1):
        for h, cols in enumerate(halves):
            home[2 * f + h].wait()
            part = unmix(f, cols)
            back_v[:, cols] = part if f == 0 else back_v[:, cols] + part
    last = []
    f = facets - 1
    for h, cols in enumerate(halves):
        home[2 * f + h].wait()
        part = unmix(f, cols)
        back_b[:, cols] = (back_v[:, cols] + part if f else part).astype(jnp.bfloat16)
        last.append(exchange(3 + 3 * facets + h, back_b, dsky, cols))
        last[h].start()

    @pl.loop(1, n)
    def _(k):
        pot_y(k).wait()

    part_x[gx] = jnp.sum(part_y[...], axis=0)

    @pl.loop(1, m)
    def _(k):
        pot_x(k).start()

    for c in last:
        c.wait()
    for a in (0, 1):
        rows = slice(a * nm, (a + 1) * nm)
        lined = f32dot(mat_m[rows, :], dsky[...], (1, 0)).astype(jnp.bfloat16)
        quad_m[rows, :] = f32dot(lined, mat_m[...], (1, 1))
    parent_terms(quad_m, cf, shift_m, res_m, nm, 16)
    halo_f = halo(2, res_m, row_f, False)
    halo_f.start()
    grad_f[...] = dsky[...].astype(jnp.float32) + xf[...]
    save_f = pltpu.make_async_copy(grad_f, g_f, save.at[0])
    save_f.start()
    halo_f.wait()
    halo_f.fold(res_m)
    dmiddle = res_m[ROW : ROW + nm, LANE : LANE + nm]
    high, low = split(dmiddle)
    for a in (0, 1):
        rows = slice(a * nc, (a + 1) * nc)
        matrix = mat_c[rows, :]
        quad_c[rows, :] = f32dot(
            f32dot(matrix, high, (1, 0)).astype(jnp.bfloat16), mat_c[...], (1, 1)
        ) + f32dot(f32dot(matrix, low, (1, 0)).astype(jnp.bfloat16), mat_c[...], (1, 1))
    parent_terms(quad_c, cm, shift_c, res_c, nc, 32)
    halo_b = halo(3, res_c, row_b, False)
    halo_b.start()
    grad_m[...] = res_m[ROW : ROW + nm, LANE : LANE + nm] + xm[...]
    save_m = pltpu.make_async_copy(grad_m, g_m, save.at[1])
    save_m.start()

    @pl.loop(1, m)
    def _(k):
        pot_x(k).wait()

    pot[0, 0] = jnp.sum(part_x[...]) / cells
    halo_b.wait()
    halo_b.fold(res_c)
    grad_c[...] = res_c[ROW : ROW + nc, LANE : LANE + nc] + pad_c[ROW : ROW + nc, LANE : LANE + nc]
    save_c = pltpu.make_async_copy(grad_c, g_c, save.at[2])
    save_c.start()
    save_f.wait()
    save_m.wait()
    save_c.wait()


def finish(*refs):
    count = (len(refs) - 2) // 3
    given, given_out, held = refs[:count], refs[count : 2 * count], refs[2 * count : 3 * count]
    come, go = refs[3 * count :]
    blocks = []
    for a, b, v in zip(given, given_out, held):
        rows = min(LANE, a.shape[0])
        for start in range(0, a.shape[0], rows):
            here = slice(start, start + rows)
            i = len(blocks)
            blocks.append(
                (
                    pltpu.make_async_copy(a.at[here, :], v.at[here, :], come.at[i]),
                    pltpu.make_async_copy(v.at[here, :], b.at[here, :], go.at[i]),
                )
            )
    for read, _ in blocks:
        read.start()
    for read, write in blocks:
        read.wait()
        write.start()
    for _, write in blocks:
        write.wait()


def body(
    xi_coarse, xi_middle, xi_fine, coef_middle, coef_fine, kern_u, kern_v, vis_data, facet_tiles, facet_weight, facet_count
):
    m, n = lax.axis_size("gx"), lax.axis_size("gy")
    nc, nm, nf = xi_coarse.shape[0], xi_middle.shape[0], xi_fine.shape[0]
    facets, bins = kern_u.shape[1], vis_data.shape[2]
    cells = float(m * n * nf * nf)
    f32, bf16 = jnp.float32, jnp.bfloat16
    vmem, dma = pltpu.VMEM, pltpu.SemaphoreType.DMA

    def wide(size):
        return vmem((size + 2 * ROW, size + 2 * LANE), f32)

    def strips(size):
        return vmem((2, ROW, size + 2 * LANE), f32)

    swaps = 5 + 3 * facets
    scratch = [
        wide(nc), wide(nm), vmem((nm, nm), f32), vmem((nf, nf), f32),
        vmem(coef_middle.shape, bf16), vmem(coef_fine.shape, bf16),
        vmem(kern_u.shape[1:], bf16), vmem(kern_v.shape[1:], bf16), vmem(vis_data.shape[1:], bf16),
        vmem((facets, nf, bins), bf16),
        vmem((nc + 2 * ROW, nc), f32), vmem((nm + 2 * ROW, nm), f32),
        vmem((9, nc, nc), f32), vmem((9, nm, nm), f32),
        vmem((nm, nm), bf16), vmem((nm, nm), bf16), vmem((nf, nf), bf16), vmem((nf, nf), bf16),
        vmem((nm // LANE, nm, LANE), f32), vmem((nf // LANE, nf, LANE), f32),
        vmem((nm, nm), bf16), vmem((nf, nf), bf16),
        vmem((8, LANE), f32), vmem((n, 8, LANE), f32), vmem((facets, nf, nf), bf16), vmem((facets, nf, nf), bf16),
        vmem((nf, nf), bf16), vmem((nf, nf), bf16), vmem((nf, LANE), bf16), vmem((nf, LANE), bf16),
        vmem((nf, nf), bf16), vmem((facets, nf, nf), bf16), vmem((facets, nf, nf), bf16),
        vmem((bins, nf), bf16), vmem((facets, nf, nf), bf16), vmem((facets, nf, nf), bf16),
        vmem((nf, nf), bf16), vmem((nf, nf), bf16),
        vmem((nm, nm), f32), vmem((nf, nf), f32),
        vmem((3, nc + 4 * ROW, nc + 2 * LANE), f32), vmem((3, nm + 4 * ROW, nm + 2 * LANE), f32),
        wide(nc), wide(nm), vmem((nc, nc), f32), vmem((nm, nm), f32), vmem((nf, nf), f32), vmem((nf, nf), f32),
        strips(nc), strips(nm), strips(nm), strips(nc), vmem((4, 2, ROW, LANE), f32), vmem((4, 2, ROW, LANE), f32),
        vmem((1, bins), f32), vmem((n, 8, LANE), f32), vmem((m, 8, LANE), f32),
        dma((8,)), dma((3,)), dma((4, 8)), dma((4, 8)),
        dma((swaps, n)), dma((swaps, n)),
        dma((n,)), dma((n,)), dma((n,)), dma((n,)), dma((m,)), dma((m,)),
    ]
    hbm = pl.BlockSpec(memory_space=pl.ANY)
    small = pl.BlockSpec(memory_space=pltpu.SMEM)
    shapes = [jax.ShapeDtypeStruct(x.shape, f32) for x in (xi_coarse, xi_middle, xi_fine)]
    *grads, total = pl.pallas_call(
        functools.partial(kernel, m, n, cells),
        name="prior_gradient",
        out_shape=(*shapes, jax.ShapeDtypeStruct((1, 1), f32)),
        in_specs=[hbm] * 8 + [small] * 3,
        out_specs=(hbm, hbm, hbm, small),
        scratch_shapes=scratch,
        compiler_params=pltpu.CompilerParams(
            collective_id=0, has_side_effects=True, vmem_limit_bytes=62 * 1024 * 1024
        ),
    )(
        xi_coarse, xi_middle, xi_fine, coef_middle, coef_fine, kern_u, kern_v, vis_data,
        facet_tiles, facet_weight, facet_count,
    )
    grads = pl.pallas_call(
        finish,
        name="hand_out",
        out_shape=shapes,
        in_specs=[hbm] * 3,
        out_specs=[hbm] * 3,
        scratch_shapes=[*[vmem(s.shape, f32) for s in shapes], dma((8,)), dma((8,))],
    )(*grads)
    return (*grads, total.reshape(()))


def solution(mesh):
    placed = (
        P("gx", "gy"),
        P("gx", "gy"),
        P("gx", "gy"),
        P(None, None, "gx", "gy"),
        P(None, None, "gx", "gy"),
        P("gx", "gy", None, None),
        P("gx", "gy", None, None),
        P("gx", "gy", None, None),
        P("gx", "gy", None),
        P("gx", "gy", None),
        P("gx", "gy"),
    )
    return jax.shard_map(
        body,
        mesh=mesh,
        in_specs=placed,
        out_specs=(P("gx", "gy"), P("gx", "gy"), P("gx", "gy"), P()),
        check_vma=False,
    )
```

time: 99.8 us -> 88.2 us (0.88)
  local copies, waits for them, and re-layouts: 6.91 us -> 0 us
  Pallas kernels: 89.5 us -> 85.8 us
    pallas_call x1, Pallas kernels: 89.5 us -> 83.5 us  [body(): pl.pallas_call(functools.partial(kernel, m, n, cells), name='prior_gradie...]
    unnamed x3 -> x0, local copies, waits for them, and re-layouts: 5.4 us -> none
    pallas_call x0 -> x1, Pallas kernels: none -> 2.22 us  [body(): pl.pallas_call(finish, name='hand_out', out_shape=shapes, in_specs=[hbm]...]
where the time goes in v2:
time: 88.2 us; the launch traced here: 88.1 us
  Pallas kernels  85.8 us (97%)
  between operations  2.32 us (3%)
    pallas_call x1, Pallas kernels, body(): pl.pallas_call(functools.partial(kernel, m, n, cells), name='prior_gradie...  83.5 us
    pallas_call x1, Pallas kernels, body(): pl.pallas_call(finish, name='hand_out', out_shape=shapes, in_specs=[hbm]...  2.22 us

profile of v2, /device:TPU:0, one launch (start us, length us, event | category | flops | bytes accessed | tf_op | source)
XLA Modules:
  0.0 88.1 jit_solution(9336826066398746071)
XLA Ops:
  0.6 83.5 %prior_gradient.1 = (f32[128,128]{1,0:T(8,128)}, f32[256,256]{1,0:T(8,128)}, f32[512,512]{1,0:T(8,128)}, f32[1,1]{1,0:T(1,128)}) custom-call(f32[128,128]{1,0:T(8,128)} %xi_c.1, f32[256,256]{1,0:T(8,128)} %xi_m.1, f32[512,512]{1,0:T(8,128)} %xi_f.1, bf16[4,9,128,128]{3,2,1,0:T(8,128)(2,1)} %co_m.1, bf16[4,9,256,256]{3,2,1,0:T(8,128)(2,1)} %co_f.1, ...), custom_call_target="tpu_custom_call" | custom-call | tf_op jit(solution)/shard_map/prior_gradient/pallas_call | solution.py:639
  84.2 2.2 %hand_out.1 = (f32[128,128]{1,0:T(8,128)}, f32[256,256]{1,0:T(8,128)}, f32[512,512]{1,0:T(8,128)}) custom-call(f32[128,128]{1,0:T(8,128)} %get-tuple-element.11.refs_0_, f32[256,256]{1,0:T(8,128)} %get-tuple-element.12.refs_1_, f32[512,512]{1,0:T(8,128)} %get-tuple-element.13.refs_2_), custom_call_target="tpu_custom_call" | custom-call | tf_op jit(solution)/shard_map/hand_out/pallas_call | solution.py:653

commit v3 on v2

--- a/solution.py
+++ b/solution.py
@@ -10,6 +10,7 @@
 inv_noise = 0.125
 MESH = pl.DeviceIdType.MESH
 ROW, LANE = 8, 128
+END = 16
 SIDES = [(dx, dy) for dx in (-1, 0, 1) for dy in (-1, 0, 1) if (dx, dy) != (0, 0)]
 
 
@@ -60,6 +61,10 @@
             )
 
     def start(self):
+        self.pack()
+        self.send()
+
+    def pack(self):
         size, eye = self.size, diagonal()
         for side, dy in ((0, 1), (1, -1)):
             lane = (LANE + size - 1 if dy > 0 else LANE) if self.near else (LANE + size if dy > 0 else LANE - 1)
@@ -68,6 +73,8 @@
                 block = self.src[ROW + b * LANE : ROW + (b + 1) * LANE, tile : tile + LANE]
                 block = jnp.broadcast_to(block[:, lane - tile : lane - tile + 1], (LANE, LANE))
                 self.cols_out[side, b : b + 1, :] = jnp.sum(jnp.where(eye, block, 0.0), axis=0, keepdims=True)
+
+    def send(self):
         for c in self.copies:
             c.start()
 
@@ -94,7 +101,10 @@
     def surround(self, pad):
         size = self.size
         for side, start in ((0, 0), (1, ROW + size)):
-            pad[start : start + ROW, :] = jnp.concatenate(self.strips(side), axis=1)
+            before, middle, after = self.strips(side)
+            before = jnp.broadcast_to(before[:, LANE - 1 : LANE], (ROW, LANE))
+            after = jnp.broadcast_to(after[:, 0:1], (ROW, LANE))
+            pad[start : start + ROW, :] = jnp.concatenate([before, middle, after], axis=1)
         for side, start in ((0, 0), (1, LANE + size)):
             pad[ROW : ROW + size, start : start + LANE] = jnp.broadcast_to(self.column(side), (size, LANE))
 
@@ -148,34 +158,19 @@
         def _(k):
             self.copy(k).wait()
 
-    def meets(self, index, ends):
-        n = self.at[3]
-        at_end = (index == 0) | (index == n - 1)
-        return at_end if ends else jnp.logical_not(at_end)
-
-    def start_some(self, low, high, ends):
-        gx, gy, m, n = self.at
-
-        @pl.loop(low, high)
-        def _(k):
-            @pl.when(self.meets(lax.rem(gy + k, n), ends))
-            def _():
-                self.copy(k).start()
-
-    def wait_some(self, ends):
-        gx, gy, m, n = self.at
-
-        @pl.loop(1, n)
-        def _(k):
-            @pl.when(self.meets(lax.rem(gy + k, n), ends))
-            def _():
-                self.copy(k).wait_send()
-
-        @pl.when(self.meets(gy, ends))
-        def _():
+    def start_ends(self):
+        gy, n = self.at[1], self.at[3]
+        self.own()
+        for ends in (True, False):
+
             @pl.loop(1, n)
             def _(k):
-                self.copy(k).wait_recv()
+                peer = lax.rem(gy + k, n)
+                at_end = (peer == 0) | (peer == n - 1)
+
+                @pl.when(at_end if ends else jnp.logical_not(at_end))
+                def _():
+                    self.copy(k).start()
 
 
 def spread(ref):
@@ -188,12 +183,15 @@
 
 
 def refine(pad, wins, coef, rolled, high, low, size, rows):
-    width = size + 2 * LANE
+    own = pad[:, LANE : LANE + size]
+    lane = lax.broadcasted_iota(jnp.int32, own.shape, 1)
     for dj in (-1, 0, 1):
-        value = pad[...]
+        value = own
         if dj:
-            value = pltpu.roll(value, (-dj) % width, 1)
-        rolled[...] = value[:, LANE : LANE + size]
+            beyond = pad[:, 0:LANE] if dj < 0 else pad[:, LANE + size : 2 * LANE + size]
+            beyond = jnp.concatenate([beyond] * (size // LANE), axis=1)
+            value = jnp.where(lane == (0 if dj < 0 else size - 1), beyond, pltpu.roll(own, (-dj) % size, 1))
+        rolled[...] = value
         for di in (-1, 0, 1):
             wins[3 * (di + 1) + dj + 1] = rolled[ROW + di : ROW + di + size, :]
 
@@ -237,18 +235,19 @@
             for a in (0, 1)
             for b in (0, 1)
         ]
-        blank = jnp.zeros((rows, LANE), jnp.float32)
+        lane = lax.broadcasted_iota(jnp.int32, (rows, size), 1)
         for d in range(3):
-            total = None
+            parts = []
             for j in range(3):
                 part = None
                 for child in range(4):
                     term = coef[child, 3 * d + j, here, :].astype(jnp.float32) * quad[child]
                     part = term if child == 0 else part + term
-                part = jnp.concatenate([blank, part, blank], axis=1)
-                if j != 1:
-                    part = pltpu.roll(part, (j - 1) % width, 1)
-                total = part if j == 0 else total + part
+                parts.append(part if j == 1 else pltpu.roll(part, (j - 1) % size, 1))
+            total = parts[1] + jnp.where(lane < size - 1, parts[0], 0.0) + jnp.where(lane > 0, parts[2], 0.0)
+            before = jnp.where(lane == size - 1, parts[0], 0.0)[:, size - LANE : size]
+            after = jnp.where(lane == 0, parts[2], 0.0)[:, 0:LANE]
+            total = jnp.concatenate([before, total, after], axis=1)
             shifted[d, pl.ds(pl.multiple_of(at + 2 * ROW, ROW), rows), :] = total
 
     high = tall - 2 * ROW
@@ -272,15 +271,15 @@
 
 def kernel(
     m, n, cells,
-    xi_c, xi_m, xi_f, co_m, co_f, k_u, k_v, v_d, listed, weights, counts,
+    xi_c, xi_m, xi_f, co_m, co_f, k_u, k_v, v_d, f_t, f_w, f_c,
     g_c, g_m, g_f, pot,
     pad_c, pad_m, xm, xf, cm, cf, ku, kv, vd, kut,
     roll_c, roll_m, win_c, win_m, hi_c, lo_c, hi_m, lo_m, lace_c, lace_m, mat_c, mat_m,
-    meta, metas, mix_hi, mix_lo, sky, sky_2, edge, edges, tiles, sums, fsum, damps, dsum, dslab, back_b, dsky,
-    quad_c, quad_m, shift_c, shift_m, res_c, res_m, grad_c, grad_m, grad_f, back_v,
+    listed, weights, counts, total_s, meta, metas, mix_hi, mix_lo, sky, sky_2, edge, edges, lates, tiles, tiles_o, sums, fsum, damps, dsum, dslab, back_b, dsky, dtile, ends,
+    quad_c, quad_m, shift_c, shift_m, res_c, res_m, res_r, grad_c, grad_m, grad_f, back_v,
     row_c, row_m, row_f, row_b, col_o, col_i,
     parts, part_y, part_x,
-    load, save, sem_s, sem_r, a2a_s, a2a_r, sem_ts, sem_tr, sem_ys, sem_yr, sem_xs, sem_xr,
+    load, few, save, sem_s, sem_r, a2a_s, a2a_r, sem_ls, sem_lr, sem_es, sem_er, sem_ts, sem_tr, sem_ys, sem_yr, sem_xs, sem_xr,
 ):
     gx, gy = lax.axis_index("gx"), lax.axis_index("gy")
     at = (gx, gy, m, n)
@@ -304,6 +303,13 @@
         pl.semaphore_signal(barrier, inc=1, device_id=(gx, lax.rem(gy + k, n)), device_id_type=MESH)
         greeted += 1
 
+    left, right, inside = slice(0, LANE), slice(nf - LANE, nf), slice(LANE, nf - LANE)
+    halves = (slice(0, 2 * LANE), slice(2 * LANE, nf))
+    moved = ((left, slice(0, LANE)), (right, slice(LANE, 2 * LANE)), (inside, halves[1]))
+    small = [
+        pltpu.make_async_copy(src, dst, few.at[i])
+        for i, (src, dst) in enumerate(((f_t, listed), (f_w, weights), (f_c, counts)))
+    ]
     loads = [
         pltpu.make_async_copy(src, dst, load.at[i])
         for i, (src, dst) in enumerate(
@@ -314,12 +320,12 @@
                 (co_f, cf),
                 (xi_f, xf),
                 (k_u.at[0], ku),
-                (k_v.at[0], kv),
+                *((k_v.at[0, :, :, natural], kv.at[:, :, put]) for natural, put in moved),
                 (v_d.at[0], vd),
             )
         )
     ]
-    for c in loads:
+    for c in loads[:3] + small + loads[3:]:
         c.start()
 
     def blank(pad, size):
@@ -353,19 +359,19 @@
     spread(mat_m)
     blank(pad_c, nc)
     blank(pad_m, nm)
+    for c in small:
+        c.wait()
     for f in range(facets):
         for s in range(2):
             i = 2 * f + s
             meta[i : i + 1, :] = jnp.full((1, LANE), listed[0, f, s].astype(jnp.float32))
             meta[4 + i : 5 + i, :] = jnp.full((1, LANE), weights[0, f, s])
-    for c in loads[:3]:
-        c.wait()
-    middle_level()
     col_o[...] = jnp.zeros_like(col_o)
+    loads[0].wait()
+    halo_c = halo(0, pad_c, row_c, True)
+    halo_c.pack()
     pl.semaphore_wait(barrier, greeted)
-
-    halo_c = halo(0, pad_c, row_c, True)
-    halo_c.start()
+    halo_c.send()
 
     def meta_copy(k):
         return pltpu.make_async_remote_copy(
@@ -382,18 +388,20 @@
         meta_copy(k).start()
 
     metas[gy] = meta[...]
+    for c in loads[1:3]:
+        c.wait()
+    middle_level()
     for c in loads[3:5]:
         c.wait()
     fine_level(sky)
     early = exchange(0, sky, tiles)
-    early.start_some(1, n // 2, False)
 
     halo_c.wait()
     halo_c.surround(pad_c)
     middle_level()
     halo_m = halo(1, pad_m, row_m, True)
     halo_m.start()
-    early.start_some(n // 2, n, False)
+    early.start()
 
     @pl.loop(1, n)
     def _(k):
@@ -417,29 +425,66 @@
                 total = total + jnp.where((tile == tile_of) & same, weight, 0.0)
             mix_hi[f, rows, :], mix_lo[f, rows, :] = split(total)
 
+    owners = ((0, 0), (1, n - 1))
+
+    def late_copy(e, owner, source):
+        return pltpu.make_async_remote_copy(
+            src_ref=sky_2.at[pl.ds(owner * slab + e * (slab - END), END), :],
+            dst_ref=lates.at[source],
+            send_sem=sem_ls.at[e],
+            recv_sem=sem_lr.at[source],
+            device_id=(gx, owner),
+            device_id_type=MESH,
+        )
+
     halo_m.wait()
     halo_m.surround(pad_m)
     fine_level(sky_2)
-    left, right = slice(0, LANE), slice(nf - LANE, nf)
     outer = lax.broadcasted_iota(jnp.int32, (nf, LANE), 1) < LANE // 2
     edge[...] = jnp.where(outer, sky_2[:, left], sky_2[:, right])
-    late = exchange(1, sky_2, tiles)
-    rim = exchange(2, edge, edges)
-    late.start_some(1, n, True)
+    rim = exchange(1, edge, edges)
+    for e, owner in owners:
+
+        @pl.when(gy != owner)
+        def _(e=e, owner=owner):
+            late_copy(e, owner, gy).start()
+
+        @pl.when(gy == owner)
+        def _(e=e, owner=owner):
+            lates[owner] = sky_2[owner * slab + e * (slab - END) : owner * slab + e * (slab - END) + END, :]
+
     rim.start()
-    late.own()
+
     prior = fold_lanes(squares(pad_c[ROW : ROW + nc, LANE : LANE + nc]))
     prior = prior + fold_lanes(squares(xm[...])) + fold_lanes(squares(xf[...]))
     parts[...] = jnp.zeros_like(parts)
-    early.wait_some(False)
-    late.wait_some(True)
+    early.wait()
+    for e, owner in owners:
+
+        @pl.when(gy != owner)
+        def _(e=e, owner=owner):
+            late_copy(e, owner, gy).wait_send()
+
+        @pl.when(gy == owner)
+        def _(e=e, owner=owner):
+            @pl.loop(1, n)
+            def _(k):
+                late_copy(e, owner, lax.rem(owner + k, n)).wait_recv()
+
+            for i in range(n):
+                at_row = i * slab + e * (slab - END)
+                tiles[at_row : at_row + END, :] = lates[i]
+
     rim.wait()
-    tiles[:, left] = jnp.where(outer, edges[...], tiles[:, left])
-    tiles[:, right] = jnp.where(outer, tiles[:, right], edges[...])
+    mixed = jnp.concatenate(
+        [jnp.where(outer, edges[...], tiles[:, left]), jnp.where(outer, tiles[:, right], edges[...]), tiles[:, inside]],
+        axis=1,
+    )
+    tiles_o[...] = mixed
     out = []
     for f in range(facets):
-        sums[f] = (f32dot(mix_hi[f], tiles[...], (1, 0)) + f32dot(mix_lo[f], tiles[...], (1, 0))).astype(jnp.bfloat16)
-        out.append(exchange(3 + f, sums.at[f], fsum.at[f]))
+        sums[f] = (f32dot(mix_hi[f], tiles_o[...], (1, 0)) + f32dot(mix_lo[f], tiles_o[...], (1, 0))).astype(jnp.bfloat16)
+        out.append(exchange(2 + f, sums.at[f], fsum.at[f]))
         out[f].start()
 
     for c in loads[5:]:
@@ -447,15 +492,13 @@
     for f in range(facets):
         kut[f] = ku[f].T
     home = []
-    chunk = 256
-    halves = [slice(h * nf // 2, (h + 1) * nf // 2) for h in (0, 1)]
+    chunk = 512
     for f in range(facets):
         out[f].wait()
         count = counts[0, f]
 
-        @pl.loop(0, bins // chunk)
-        def _(step):
-            here = pl.ds(pl.multiple_of(step * chunk, chunk), chunk)
+        for step in range(bins // chunk):
+            here = slice(step * chunk, (step + 1) * chunk)
             amp = f32dot(ku[f, here, :], fsum[f], (1, 0)).astype(jnp.bfloat16)
             vis = f32dot(amp, kv[f], (1, 1))
             bin_at = step * chunk + lax.broadcasted_iota(jnp.int32, (chunk, bins), 0)
@@ -466,8 +509,12 @@
 
         for h, cols in enumerate(halves):
             dsum[f, :, cols] = f32dot(kut[f], damps[:, cols], (1, 0)).astype(jnp.bfloat16)
-            home.append(exchange(3 + facets + 2 * f + h, dsum.at[f], dslab.at[f], cols))
-            home[-1].start()
+            going = exchange(2 + facets + 2 * f + h, dsum.at[f], dslab.at[f], cols)
+            home.append(going)
+            if f < facets - 1 or h == 0:
+                going.start()
+            else:
+                going.start_ends()
 
     own = 0.5 * prior + 0.5 * inv_noise * fold_lanes(parts[...])
     part_y[gy] = jnp.where(lax.broadcasted_iota(jnp.int32, (ROW, LANE), 0) == 0, own, 0.0)
@@ -504,13 +551,53 @@
             home[2 * f + h].wait()
             part = unmix(f, cols)
             back_v[:, cols] = part if f == 0 else back_v[:, cols] + part
+    def ends_copy(e, k):
+        peer = lax.rem(gy + k, n)
+        return pltpu.make_async_remote_copy(
+            src_ref=back_b.at[ends_rows(e, peer), halves[1]],
+            dst_ref=ends.at[e],
+            send_sem=sem_es.at[e, k],
+            recv_sem=sem_er.at[e, k],
+            device_id=(gx, peer),
+            device_id_type=MESH,
+        )
+
+    def ends_rows(e, index):
+        return pl.ds(pl.multiple_of(index * slab + e * (slab - END), END), END)
+
+    def ends_start():
+        for e, owner in owners:
+
+            @pl.when(gy == owner)
+            def _(e=e):
+                @pl.loop(1, n)
+                def _(k):
+                    ends_copy(e, k).start()
+
+                ends[e] = back_b[ends_rows(e, gy), halves[1]]
+
+    def ends_wait():
+        for e, owner in owners:
+
+            @pl.when(gy == owner)
+            def _(e=e):
+                @pl.loop(1, n)
+                def _(k):
+                    ends_copy(e, k).wait_send()
+
+            @pl.when(gy != owner)
+            def _(e=e, owner=owner):
+                ends_copy(e, lax.rem(gy - owner + n, n)).wait_recv()
+
     last = []
     f = facets - 1
     for h, cols in enumerate(halves):
         home[2 * f + h].wait()
         part = unmix(f, cols)
         back_b[:, cols] = (back_v[:, cols] + part if f else part).astype(jnp.bfloat16)
-        last.append(exchange(3 + 3 * facets + h, back_b, dsky, cols))
+        if h:
+            ends_start()
+        last.append(exchange(2 + 3 * facets + h, back_b, dsky, cols))
         last[h].start()
 
     @pl.loop(1, n)
@@ -523,16 +610,27 @@
     def _(k):
         pot_x(k).start()
 
-    for c in last:
-        c.wait()
-    for a in (0, 1):
-        rows = slice(a * nm, (a + 1) * nm)
-        lined = f32dot(mat_m[rows, :], dsky[...], (1, 0)).astype(jnp.bfloat16)
-        quad_m[rows, :] = f32dot(lined, mat_m[...], (1, 1))
-    parent_terms(quad_m, cf, shift_m, res_m, nm, 16)
-    halo_f = halo(2, res_m, row_f, False)
+    def adjoint_fine(result):
+        for a in (0, 1):
+            rows = slice(a * nm, (a + 1) * nm)
+            lined = f32dot(mat_m[rows, :], dtile[...], (1, 0)).astype(jnp.bfloat16)
+            quad_m[rows, :] = f32dot(lined, mat_m[...], (1, 1))
+        parent_terms(quad_m, cf, shift_m, result, nm, 16)
+
+    last[0].wait()
+    dtile[:, left] = dsky[:, 0:LANE]
+    dtile[:, right] = dsky[:, LANE : 2 * LANE]
+    dtile[END : nf - END, inside] = jnp.zeros((nf - 2 * END, nf - 2 * LANE), jnp.bfloat16)
+    ends_wait()
+    dtile[0:END, inside] = ends[0]
+    dtile[nf - END : nf, inside] = ends[1]
+    adjoint_fine(res_r)
+    halo_f = halo(2, res_r, row_f, False)
     halo_f.start()
-    grad_f[...] = dsky[...].astype(jnp.float32) + xf[...]
+    last[1].wait()
+    dtile[:, inside] = dsky[:, halves[1]]
+    adjoint_fine(res_m)
+    grad_f[...] = dtile[...].astype(jnp.float32) + xf[...]
     save_f = pltpu.make_async_copy(grad_f, g_f, save.at[0])
     save_f.start()
     halo_f.wait()
@@ -556,7 +654,9 @@
     def _(k):
         pot_x(k).wait()
 
-    pot[0, 0] = jnp.sum(part_x[...]) / cells
+    total_s[0, 0] = jnp.sum(part_x[...]) / cells
+    save_p = pltpu.make_async_copy(total_s, pot, save.at[3])
+    save_p.start()
     halo_b.wait()
     halo_b.fold(res_c)
     grad_c[...] = res_c[ROW : ROW + nc, LANE : LANE + nc] + pad_c[ROW : ROW + nc, LANE : LANE + nc]
@@ -565,6 +665,7 @@
     save_f.wait()
     save_m.wait()
     save_c.wait()
+    save_p.wait()
 
 
 def finish(*refs):
@@ -608,7 +709,7 @@
     def strips(size):
         return vmem((2, ROW, size + 2 * LANE), f32)
 
-    swaps = 5 + 3 * facets
+    swaps = 4 + 3 * facets
     scratch = [
         wide(nc), wide(nm), vmem((nm, nm), f32), vmem((nf, nf), f32),
         vmem(coef_middle.shape, bf16), vmem(coef_fine.shape, bf16),
@@ -619,29 +720,31 @@
         vmem((nm, nm), bf16), vmem((nm, nm), bf16), vmem((nf, nf), bf16), vmem((nf, nf), bf16),
         vmem((nm // LANE, nm, LANE), f32), vmem((nf // LANE, nf, LANE), f32),
         vmem((nm, nm), bf16), vmem((nf, nf), bf16),
+        pltpu.SMEM(facet_tiles.shape, jnp.int32), pltpu.SMEM(facet_weight.shape, f32),
+        pltpu.SMEM(facet_count.shape, jnp.int32), pltpu.SMEM((1, 1), f32),
         vmem((8, LANE), f32), vmem((n, 8, LANE), f32), vmem((facets, nf, nf), bf16), vmem((facets, nf, nf), bf16),
         vmem((nf, nf), bf16), vmem((nf, nf), bf16), vmem((nf, LANE), bf16), vmem((nf, LANE), bf16),
-        vmem((nf, nf), bf16), vmem((facets, nf, nf), bf16), vmem((facets, nf, nf), bf16),
+        vmem((n, END, nf), bf16), vmem((nf, nf), bf16), vmem((nf, nf), bf16),
+        vmem((facets, nf, nf), bf16), vmem((facets, nf, nf), bf16),
         vmem((bins, nf), bf16), vmem((facets, nf, nf), bf16), vmem((facets, nf, nf), bf16),
-        vmem((nf, nf), bf16), vmem((nf, nf), bf16),
+        vmem((nf, nf), bf16), vmem((nf, nf), bf16), vmem((nf, nf), bf16), vmem((2, END, nf - 2 * LANE), bf16),
         vmem((nm, nm), f32), vmem((nf, nf), f32),
         vmem((3, nc + 4 * ROW, nc + 2 * LANE), f32), vmem((3, nm + 4 * ROW, nm + 2 * LANE), f32),
-        wide(nc), wide(nm), vmem((nc, nc), f32), vmem((nm, nm), f32), vmem((nf, nf), f32), vmem((nf, nf), f32),
+        wide(nc), wide(nm), wide(nm), vmem((nc, nc), f32), vmem((nm, nm), f32), vmem((nf, nf), f32), vmem((nf, nf), f32),
         strips(nc), strips(nm), strips(nm), strips(nc), vmem((4, 2, ROW, LANE), f32), vmem((4, 2, ROW, LANE), f32),
         vmem((1, bins), f32), vmem((n, 8, LANE), f32), vmem((m, 8, LANE), f32),
-        dma((8,)), dma((3,)), dma((4, 8)), dma((4, 8)),
-        dma((swaps, n)), dma((swaps, n)),
+        dma((10,)), dma((3,)), dma((4,)), dma((4, 8)), dma((4, 8)),
+        dma((swaps, n)), dma((swaps, n)), dma((2,)), dma((n,)), dma((2, n)), dma((2, n)),
         dma((n,)), dma((n,)), dma((n,)), dma((n,)), dma((m,)), dma((m,)),
     ]
     hbm = pl.BlockSpec(memory_space=pl.ANY)
-    small = pl.BlockSpec(memory_space=pltpu.SMEM)
     shapes = [jax.ShapeDtypeStruct(x.shape, f32) for x in (xi_coarse, xi_middle, xi_fine)]
     *grads, total = pl.pallas_call(
         functools.partial(kernel, m, n, cells),
         name="prior_gradient",
         out_shape=(*shapes, jax.ShapeDtypeStruct((1, 1), f32)),
-        in_specs=[hbm] * 8 + [small] * 3,
-        out_specs=(hbm, hbm, hbm, small),
+        in_specs=[hbm] * 11,
+        out_specs=[hbm] * 4,
         scratch_shapes=scratch,
         compiler_params=pltpu.CompilerParams(
             collective_id=0, has_side_effects=True, vmem_limit_bytes=62 * 1024 * 1024

time: 88.2 us -> 84.8 us (0.961)
  Pallas kernels: 85.8 us -> 82.3 us
    pallas_call x1, Pallas kernels: 83.5 us -> 80.1 us  [body(): pl.pallas_call(functools.partial(kernel, m, n, cells), name='prior_gradie...]
where the time goes in v3:
time: 84.8 us; the launch traced here: 84.6 us
  Pallas kernels  82.3 us (97%)
  between operations  2.32 us (3%)
    pallas_call x1, Pallas kernels, body(): pl.pallas_call(functools.partial(kernel, m, n, cells), name='prior_gradie...  80.1 us
    pallas_call x1, Pallas kernels, body(): pl.pallas_call(finish, name='hand_out', out_shape=shapes, in_specs=[hbm]...  2.22 us

profile of v3, /device:TPU:0, one launch (start us, length us, event | category | flops | bytes accessed | tf_op | source)
XLA Modules:
  0.0 84.6 jit_solution(6298011320015334647)
XLA Ops:
  0.6 80.1 %prior_gradient.1 = (f32[128,128]{1,0:T(8,128)}, f32[256,256]{1,0:T(8,128)}, f32[512,512]{1,0:T(8,128)}, f32[1,1]{1,0:T(1,128)}) custom-call(f32[128,128]{1,0:T(8,128)} %xi_c.1, f32[256,256]{1,0:T(8,128)} %xi_m.1, f32[512,512]{1,0:T(8,128)} %xi_f.1, bf16[4,9,128,128]{3,2,1,0:T(8,128)(2,1)} %co_m.1, bf16[4,9,256,256]{3,2,1,0:T(8,128)(2,1)} %co_f.1, ...), custom_call_target="tpu_custom_call" | custom-call | tf_op jit(solution)/shard_map/prior_gradient/pallas_call | solution.py:742
  80.7 2.2 %hand_out.1 = (f32[128,128]{1,0:T(8,128)}, f32[256,256]{1,0:T(8,128)}, f32[512,512]{1,0:T(8,128)}) custom-call(f32[128,128]{1,0:T(8,128)} %get-tuple-element.11.refs_0_, f32[256,256]{1,0:T(8,128)} %get-tuple-element.12.refs_1_, f32[512,512]{1,0:T(8,128)} %get-tuple-element.13.refs_2_), custom_call_target="tpu_custom_call" | custom-call | tf_op jit(solution)/shard_map/hand_out/pallas_call | solution.py:756

commit v4 on v3

--- a/solution.py
+++ b/solution.py
@@ -258,6 +258,56 @@
     )
 
 
+def rim_terms(quads, coef, shifted, result, size, rows):
+    width = size + 2 * LANE
+    tall = size + 4 * ROW
+    for d in range(3):
+        shifted[d, 0 : 2 * ROW, :] = jnp.zeros((2 * ROW, width), jnp.float32)
+        shifted[d, tall - 2 * ROW : tall, :] = jnp.zeros((2 * ROW, width), jnp.float32)
+
+    def term(near, at, start, length):
+        here = pl.ds(at, rows)
+        total = None
+        for child in range(4):
+            row = pl.ds(pl.multiple_of(child // 2 * size + at, rows), rows)
+            column = child % 2 * size + start
+            part = coef[child, near, here, start : start + length].astype(jnp.float32) * quads[row, column : column + length]
+            total = part if child == 0 else total + part
+        return total
+
+    @pl.loop(0, size // rows)
+    def _(step):
+        at = pl.multiple_of(step * rows, rows)
+        lane = lax.broadcasted_iota(jnp.int32, (rows, LANE), 1)
+        for d in range(3):
+            for j, start, edge, put in ((0, 0, 0, 0), (2, size - LANE, LANE - 1, LANE + size)):
+                part = jnp.where(lane == edge, term(3 * d + j, at, start, LANE), 0.0)
+                shifted[d, pl.ds(pl.multiple_of(at + 2 * ROW, ROW), rows), put : put + LANE] = pltpu.roll(
+                    part, (j - 1) % LANE, 1
+                )
+
+    lane = lax.broadcasted_iota(jnp.int32, (rows, size), 1)
+    for d, at in ((0, 0), (2, size - rows)):
+        before = pltpu.roll(term(3 * d, at, 0, size), size - 1, 1)
+        after = pltpu.roll(term(3 * d + 2, at, 0, size), 1, 1)
+        total = term(3 * d + 1, at, 0, size) + jnp.where(lane < size - 1, before, 0.0) + jnp.where(lane > 0, after, 0.0)
+        shifted[d, at + 2 * ROW : at + 2 * ROW + rows, LANE : LANE + size] = total
+
+    def summed(start, length, cols):
+        at = start + ROW
+        return (
+            shifted[1, at : at + length, cols]
+            + shifted[2, at - 1 : at - 1 + length, cols]
+            + shifted[0, at + 1 : at + 1 + length, cols]
+        )
+
+    for start in (0, ROW + size):
+        result[start : start + ROW, :] = summed(start, ROW, slice(0, width))
+    for start in (0, LANE + size):
+        cols = slice(start, start + LANE)
+        result[ROW : ROW + size, cols] = summed(ROW, size, cols)
+
+
 def squares(x):
     return jnp.sum(x * x, axis=0, keepdims=True)
 
@@ -275,7 +325,7 @@
     g_c, g_m, g_f, pot,
     pad_c, pad_m, xm, xf, cm, cf, ku, kv, vd, kut,
     roll_c, roll_m, win_c, win_m, hi_c, lo_c, hi_m, lo_m, lace_c, lace_m, mat_c, mat_m,
-    listed, weights, counts, total_s, meta, metas, mix_hi, mix_lo, sky, sky_2, edge, edges, lates, tiles, tiles_o, sums, fsum, damps, dsum, dslab, back_b, dsky, dtile, ends,
+    listed, weights, counts, total_s, meta, metas, mix_hi, mix_lo, sky, sky_2, edge, edges, late, lates, tiles, tiles_o, sums, fsum, damps, dsum, dslab, back_b, dsky, dtile, ends,
     quad_c, quad_m, shift_c, shift_m, res_c, res_m, res_r, grad_c, grad_m, grad_f, back_v,
     row_c, row_m, row_f, row_b, col_o, col_i,
     parts, part_y, part_x,
@@ -429,7 +479,7 @@
 
     def late_copy(e, owner, source):
         return pltpu.make_async_remote_copy(
-            src_ref=sky_2.at[pl.ds(owner * slab + e * (slab - END), END), :],
+            src_ref=late.at[e],
             dst_ref=lates.at[source],
             send_sem=sem_ls.at[e],
             recv_sem=sem_lr.at[source],
@@ -444,6 +494,9 @@
     edge[...] = jnp.where(outer, sky_2[:, left], sky_2[:, right])
     rim = exchange(1, edge, edges)
     for e, owner in owners:
+        start = owner * slab + e * (slab - END)
+        rows = sky_2[start : start + END, :].astype(jnp.float32)[e * ROW : (e + 1) * ROW, :]
+        late[e] = jnp.concatenate([rows[:, 0 : nf // 2], rows[:, nf // 2 : nf]], axis=0).astype(jnp.bfloat16)
 
         @pl.when(gy != owner)
         def _(e=e, owner=owner):
@@ -451,7 +504,7 @@
 
         @pl.when(gy == owner)
         def _(e=e, owner=owner):
-            lates[owner] = sky_2[owner * slab + e * (slab - END) : owner * slab + e * (slab - END) + END, :]
+            lates[owner] = late[e]
 
     rim.start()
 
@@ -473,7 +526,11 @@
 
             for i in range(n):
                 at_row = i * slab + e * (slab - END)
-                tiles[at_row : at_row + END, :] = lates[i]
+                new = lates[i].astype(jnp.float32)
+                new = jnp.concatenate([new[0:ROW, :], new[ROW : 2 * ROW, :]], axis=1)
+                old = tiles[at_row : at_row + END, :].astype(jnp.float32)
+                pair = [old[0:ROW, :], new] if e else [new, old[ROW:END, :]]
+                tiles[at_row : at_row + END, :] = jnp.concatenate(pair, axis=0).astype(jnp.bfloat16)
 
     rim.wait()
     mixed = jnp.concatenate(
@@ -610,12 +667,12 @@
     def _(k):
         pot_x(k).start()
 
-    def adjoint_fine(result):
+    def adjoint_fine(terms, result):
         for a in (0, 1):
             rows = slice(a * nm, (a + 1) * nm)
             lined = f32dot(mat_m[rows, :], dtile[...], (1, 0)).astype(jnp.bfloat16)
             quad_m[rows, :] = f32dot(lined, mat_m[...], (1, 1))
-        parent_terms(quad_m, cf, shift_m, result, nm, 16)
+        terms(quad_m, cf, shift_m, result, nm, 16)
 
     last[0].wait()
     dtile[:, left] = dsky[:, 0:LANE]
@@ -624,12 +681,12 @@
     ends_wait()
     dtile[0:END, inside] = ends[0]
     dtile[nf - END : nf, inside] = ends[1]
-    adjoint_fine(res_r)
+    adjoint_fine(rim_terms, res_r)
     halo_f = halo(2, res_r, row_f, False)
     halo_f.start()
     last[1].wait()
     dtile[:, inside] = dsky[:, halves[1]]
-    adjoint_fine(res_m)
+    adjoint_fine(parent_terms, res_m)
     grad_f[...] = dtile[...].astype(jnp.float32) + xf[...]
     save_f = pltpu.make_async_copy(grad_f, g_f, save.at[0])
     save_f.start()
@@ -724,7 +781,7 @@
         pltpu.SMEM(facet_count.shape, jnp.int32), pltpu.SMEM((1, 1), f32),
         vmem((8, LANE), f32), vmem((n, 8, LANE), f32), vmem((facets, nf, nf), bf16), vmem((facets, nf, nf), bf16),
         vmem((nf, nf), bf16), vmem((nf, nf), bf16), vmem((nf, LANE), bf16), vmem((nf, LANE), bf16),
-        vmem((n, END, nf), bf16), vmem((nf, nf), bf16), vmem((nf, nf), bf16),
+        vmem((2, END, nf // 2), bf16), vmem((n, END, nf // 2), bf16), vmem((nf, nf), bf16), vmem((nf, nf), bf16),
         vmem((facets, nf, nf), bf16), vmem((facets, nf, nf), bf16),
         vmem((bins, nf), bf16), vmem((facets, nf, nf), bf16), vmem((facets, nf, nf), bf16),
         vmem((nf, nf), bf16), vmem((nf, nf), bf16), vmem((nf, nf), bf16), vmem((2, END, nf - 2 * LANE), bf16),

time: 84.8 us -> 84.1 us (level)
  no operation moved by 1% of the time
where the time goes in v4:
time: 84.1 us; the launch traced here: 83.9 us
  Pallas kernels  81.6 us (97%)
  between operations  2.32 us (3%)
    pallas_call x1, Pallas kernels, body(): pl.pallas_call(functools.partial(kernel, m, n, cells), name='prior_gradie...  79.4 us
    pallas_call x1, Pallas kernels, body(): pl.pallas_call(finish, name='hand_out', out_shape=shapes, in_specs=[hbm]...  2.22 us

profile of v4, /device:TPU:0, one launch (start us, length us, event | category | flops | bytes accessed | tf_op | source)
XLA Modules:
  0.0 83.9 jit_solution(8762747889292850732)
XLA Ops:
  0.6 79.4 %prior_gradient.1 = (f32[128,128]{1,0:T(8,128)}, f32[256,256]{1,0:T(8,128)}, f32[512,512]{1,0:T(8,128)}, f32[1,1]{1,0:T(1,128)}) custom-call(f32[128,128]{1,0:T(8,128)} %xi_c.1, f32[256,256]{1,0:T(8,128)} %xi_m.1, f32[512,512]{1,0:T(8,128)} %xi_f.1, bf16[4,9,128,128]{3,2,1,0:T(8,128)(2,1)} %co_m.1, bf16[4,9,256,256]{3,2,1,0:T(8,128)(2,1)} %co_f.1, ...), custom_call_target="tpu_custom_call" | custom-call | tf_op jit(solution)/shard_map/prior_gradient/pallas_call | solution.py:799
  80.0 2.2 %hand_out.1 = (f32[128,128]{1,0:T(8,128)}, f32[256,256]{1,0:T(8,128)}, f32[512,512]{1,0:T(8,128)}) custom-call(f32[128,128]{1,0:T(8,128)} %get-tuple-element.11.refs_0_, f32[256,256]{1,0:T(8,128)} %get-tuple-element.12.refs_1_, f32[512,512]{1,0:T(8,128)} %get-tuple-element.13.refs_2_), custom_call_target="tpu_custom_call" | custom-call | tf_op jit(solution)/shard_map/hand_out/pallas_call | solution.py:813

commit v5 on v4

--- a/solution.py
+++ b/solution.py
@@ -601,7 +601,7 @@
         pot_y(k).start()
 
     def unmix(f, cols):
-        return f32dot(mix_hi[f], dslab[f, :, cols], (0, 0)) + f32dot(mix_lo[f], dslab[f, :, cols], (0, 0))
+        return f32dot(mix_hi[f], dslab[f, :, cols], (0, 0))
 
     for f in range(facets - 1):
         for h, cols in enumerate(halves):

time: 84.1 us -> 83.7 us (level)
  no operation moved by 1% of the time
where the time goes in v5:
time: 83.7 us; the launch traced here: 83.6 us
  Pallas kernels  81.3 us (97%)
  between operations  2.32 us (3%)
    pallas_call x1, Pallas kernels, body(): pl.pallas_call(functools.partial(kernel, m, n, cells), name='prior_gradie...  79.1 us
    pallas_call x1, Pallas kernels, body(): pl.pallas_call(finish, name='hand_out', out_shape=shapes, in_specs=[hbm]...  2.22 us

profile of v5, /device:TPU:0, one launch (start us, length us, event | category | flops | bytes accessed | tf_op | source)
XLA Modules:
  0.0 83.6 jit_solution(5446474307243381647)
XLA Ops:
  0.6 79.1 %prior_gradient.1 = (f32[128,128]{1,0:T(8,128)}, f32[256,256]{1,0:T(8,128)}, f32[512,512]{1,0:T(8,128)}, f32[1,1]{1,0:T(1,128)}) custom-call(f32[128,128]{1,0:T(8,128)} %xi_c.1, f32[256,256]{1,0:T(8,128)} %xi_m.1, f32[512,512]{1,0:T(8,128)} %xi_f.1, bf16[4,9,128,128]{3,2,1,0:T(8,128)(2,1)} %co_m.1, bf16[4,9,256,256]{3,2,1,0:T(8,128)(2,1)} %co_f.1, ...), custom_call_target="tpu_custom_call" | custom-call | tf_op jit(solution)/shard_map/prior_gradient/pallas_call | solution.py:799
  79.7 2.2 %hand_out.1 = (f32[128,128]{1,0:T(8,128)}, f32[256,256]{1,0:T(8,128)}, f32[512,512]{1,0:T(8,128)}) custom-call(f32[128,128]{1,0:T(8,128)} %get-tuple-element.11.refs_0_, f32[256,256]{1,0:T(8,128)} %get-tuple-element.12.refs_1_, f32[512,512]{1,0:T(8,128)} %get-tuple-element.13.refs_2_), custom_call_target="tpu_custom_call" | custom-call | tf_op jit(solution)/shard_map/hand_out/pallas_call | solution.py:813
